TPU v7x, 32 devices: a whole 2x2x4 slice. The times are simulated.
32 devices in a mesh: group: 2 (over y), seq: 4 (over z), member: 4 (over x, core).
Axes of the slice: x: 2, y: 2, z: 4, core: 2. Of those that a mesh axis runs over, the one named last changes fastest.
Arguments:
- tokens: bfloat16 [8, 2048, 1024], P(('group', 'member'), 'seq'), parts along dimension 0, may hold values from -6 to 6
- input_weight: bfloat16 [1024, 3072], replicated, may hold values from -0.1875 to 0.1875
- output_weight: bfloat16 [1024, 1024], replicated, may hold values from -0.75 to 0.75
- decoder_weight: bfloat16 [1024, 128], replicated, may hold values from -0.1875 to 0.1875
- neighbours: int32 [4096, 4], P('seq'), may hold values from 0 to 2047, as said below
- observed: float32 [8192, 128], P(('group', 'seq')), parts along dimension 0, may hold values from -6 to 6
- cell_area: float32 [4096], P('seq'), may hold values from 0.3 to 3
Outputs:
- attention_cotangent: bfloat16 [8, 2048, 1024], P(('group', 'member'), 'seq'), parts along dimension 0
- output_gradient: float32 [2048, 1024], P(('group', 'seq')), parts along dimension 0
- decoder_gradient: float32 [2048, 128], P('group'), parts along dimension 0
There are 2 independent parts, one for each index of `group`. A program takes and returns all parts, laid end to end along the dimension named above; an argument that names none is the same for every part. Nothing has to cross between parts.
Inputs may be any that keep to these rules, and one draw needn't show every extreme that they name: `neighbours`: the grid points held by index s of seq (rows s * 1024 to (s + 1) * 1024 - 1) name only tokens from s * 512 - 128 to (s + 1) * 512 + 127, cut to the tokens that exist; both ends of that range are named in every such block.
All inputs are finite; a program needn't handle non-finite values.
Results may differ from a plain program's by a relative error of at most 0.014.
Values may be sent and summed in bfloat16 or wider, within the bound.
A program may use at most 128 MiB of HBM per device.

v0:
```python
import math

import jax
import jax.numpy as jnp
from jax import lax
from jax.sharding import PartitionSpec as P

HEAD_DIM = 64
WINDOW = 512
REACH = 128


smooth = 0.1


def extended(cells, sides, width):
    for axis, dim in sides:
        count = lax.axis_size(axis)
        ends = count - 1
        head = lax.slice_in_dim(cells, 0, width, axis=dim)
        tail = lax.slice_in_dim(cells, cells.shape[dim] - width, cells.shape[dim], axis=dim)
        cells = jnp.concatenate(
            [
                lax.ppermute(tail, axis, [(i, (i + 1) % count) for i in range(ends)]),
                cells,
                lax.ppermute(head, axis, [((i + 1) % count, i) for i in range(ends)]),
            ],
            axis=dim,
        )
    return cells


def normalize(rows):
    values = rows.astype(jnp.float32)
    centre = jnp.mean(values, axis=-1, keepdims=True)
    spread = jnp.mean((values - centre) ** 2, axis=-1, keepdims=True)
    return ((values - centre) * lax.rsqrt(spread + 1e-05)).astype(jnp.bfloat16)


def head_norm(part):
    return (part * lax.rsqrt(jnp.mean(part * part, axis=-1, keepdims=True) + 1e-06)).astype(
        jnp.bfloat16
    )


def project(own_tokens, input_weight):
    length, width = own_tokens.shape
    heads = width // HEAD_DIM
    mixed = jnp.dot(normalize(own_tokens), input_weight, preferred_element_type=jnp.float32)
    query = head_norm(mixed[:, :width].reshape(length, heads, HEAD_DIM))
    keys = head_norm(mixed[:, width : 2 * width].reshape(length, heads, HEAD_DIM))
    values = mixed[:, 2 * width :].reshape(length, heads, HEAD_DIM).astype(jnp.bfloat16)
    return (query, keys, values)


def attend(query, keys, values, key_base, total):
    length, heads, depth = query.shape
    half = (keys.shape[0] - length) // 2
    block = min(length, max(8, 512 // heads))
    count = length // block
    scale = depth ** (-0.5)

    def one_block(index):
        start = index * block
        query_block = lax.dynamic_slice_in_dim(query, start, block, 0)
        key_block = lax.dynamic_slice_in_dim(keys, start, block + 2 * half, 0)
        value_block = lax.dynamic_slice_in_dim(values, start, block + 2 * half, 0)
        scores = (
            jnp.einsum("qhe,khe->hqk", query_block, key_block, preferred_element_type=jnp.float32)
            * scale
        )
        query_place = jnp.arange(block, dtype=jnp.int32)[:, None]
        key_place = jnp.arange(block + 2 * half, dtype=jnp.int32)[None, :]
        relative = key_place - query_place
        position = key_base + start + key_place
        valid = (relative >= 0) & (relative < 2 * half) & (position >= 0) & (position < total)
        weights = jnp.where(valid[None], jnp.exp(scores), 0.0)
        shares = (weights / jnp.sum(weights, axis=-1, keepdims=True)).astype(jnp.bfloat16)
        return jnp.einsum(
            "hqk,khe->qhe", shares, value_block, preferred_element_type=jnp.float32
        ).astype(jnp.bfloat16)

    result = lax.map(one_block, jnp.arange(count, dtype=jnp.int32))
    return result.reshape(length, heads, depth)


def slope(diff):
    return diff * lax.rsqrt(diff * diff + smooth * smooth)


def ensemble_cotangent(own, every, observed, cell_area):
    members = every.shape[0]
    pairs = jnp.sum(slope(own[..., None, :, :] - every), axis=-3)
    single = slope(own - observed)
    return (cell_area[:, None] * (single / members - pairs / (members * (members - 1)))).astype(
        jnp.bfloat16
    )


def body(tokens, input_weight, output_weight, decoder_weight, neighbours, observed, cell_area):
    own_tokens = tokens[0]
    tok_rows, width = own_tokens.shape
    seq_count = lax.axis_size("seq")
    members = lax.axis_size("member")
    seq_place = lax.axis_index("seq")
    half = WINDOW // 2
    reach = REACH
    fan_count = neighbours.shape[1]
    query, keys, values = project(own_tokens, input_weight)
    stacked = jnp.stack([query, keys, values], axis=1).reshape(tok_rows, 3, width)
    spread_heads = lax.all_to_all(stacked, "seq", split_axis=2, concat_axis=0, tiled=True)
    total = spread_heads.shape[0]
    parted = spread_heads.reshape(total, 3, -1, HEAD_DIM)
    padding = jnp.zeros((half,) + parted.shape[2:], jnp.bfloat16)
    key_full = jnp.concatenate([padding, parted[:, 1], padding], axis=0)
    value_full = jnp.concatenate([padding, parted[:, 2], padding], axis=0)
    head_result = attend(parted[:, 0], key_full, value_full, -half, total).reshape(total, -1)
    attended = lax.all_to_all(head_result, "seq", split_axis=0, concat_axis=1, tiled=True)
    latent = (
        own_tokens.astype(jnp.float32)
        + jnp.dot(attended, output_weight, preferred_element_type=jnp.float32)
    ).astype(jnp.bfloat16)
    latent_wide = extended(latent, (("seq", 0),), reach)
    local = neighbours - (seq_place * tok_rows - reach)
    pooled = (jnp.sum(latent_wide[local].astype(jnp.float32), axis=1) / fan_count).astype(
        jnp.bfloat16
    )
    fields = jnp.dot(pooled, decoder_weight, preferred_element_type=jnp.float32)
    every = lax.all_gather(fields[None], "member", axis=0, tiled=True)
    field_cotangent = ensemble_cotangent(fields, every, observed, cell_area)
    grid_total = observed.shape[0] * seq_count
    decoder_term = jnp.dot(pooled.T, field_cotangent, preferred_element_type=jnp.float32)
    decoder_gradient = lax.psum(decoder_term, ("seq", "member")) / math.sqrt(members * grid_total)
    pooled_cotangent = jnp.dot(
        field_cotangent, decoder_weight.T, preferred_element_type=jnp.float32
    )
    share = pooled_cotangent / fan_count
    wide_cotangent = jnp.zeros((tok_rows + 2 * reach, width), jnp.float32)
    for column in range(fan_count):
        wide_cotangent = wide_cotangent.at[local[:, column]].add(share)
    edges = jnp.concatenate([wide_cotangent[:reach], wide_cotangent[reach + tok_rows :]], axis=0)
    arrived = extended(edges.astype(jnp.bfloat16), (("seq", 0),), reach).astype(edges.dtype)
    own_cotangent = wide_cotangent[reach : reach + tok_rows]
    own_cotangent = own_cotangent.at[:reach].add(arrived[:reach])
    own_cotangent = own_cotangent.at[tok_rows - reach :].add(arrived[arrived.shape[0] - reach :])
    latent_cotangent = own_cotangent.astype(jnp.bfloat16)
    shard = lax.psum_scatter(
        jnp.dot(attended.T, latent_cotangent, preferred_element_type=jnp.float32).astype(
            jnp.bfloat16
        ),
        "seq",
        scatter_dimension=0,
        tiled=True,
    ).astype(jnp.float32)
    shard = lax.psum(shard.astype(jnp.bfloat16), "member").astype(jnp.float32)
    output_gradient = shard / math.sqrt(members * tok_rows * seq_count)
    attention_cotangent = jnp.dot(
        latent_cotangent, output_weight.T, preferred_element_type=jnp.float32
    ).astype(jnp.bfloat16)
    return (attention_cotangent[None], output_gradient, decoder_gradient)


def solution(mesh):
    in_specs = (
        P(("group", "member"), "seq", None),
        P(),
        P(),
        P(),
        P("seq", None),
        P(("group", "seq"), None),
        P("seq"),
    )
    out_specs = (P(("group", "member"), "seq", None), P(("group", "seq"), None), P("group", None))
    return jax.shard_map(body, mesh=mesh, in_specs=in_specs, out_specs=out_specs, check_vma=False)
```

profile of v0, /device:TPU:0, one launch (start us, length us, event | category | flops | bytes accessed | tf_op | source)
XLA Modules:
  0.0 641.5 jit_solution(11956491369685197481)
XLA Ops:
  10.4 6.1 fusion.42
  16.7 2.8 slice_multiply_fusion.1
  20.6 2.9 copy.19
  27.0 2.9 copy.20
  29.9 2.9 copy.21
  36.2 3.0 copy.22
  39.2 4.2 fusion.39
  45.4 7.6 %copy.23 = bf16[512,3,1024]{0,1,2:T(4,128)(2,1)} copy(bf16[512,3,1024]{2,0,1:T(8,128)(2,1)} %pad_maximum_fusion) | data formatting | bytes 6291456 | tf_op jit(solution)/shard_map/stack | solution.py:110
  53.0 6.5 %all-to-all-start = ((bf16[512,3,1024]{0,1,2:T(4,128)(2,1)}), bf16[512,3,1024]{0,1,2:T(4,128)(2,1)}, u32[]{:S(2)}, u32[]{:S(2)}) async-start(bf16[512,3,1024]{0,1,2:T(4,128)(2,1)} %copy.23), calls=%async_computation | async-start | bytes 8388608 | tf_op jit(solution)/shard_map/all_to_all | solution.py:111
  59.5 93.4 %all-to-all-done = bf16[512,3,1024]{0,1,2:T(4,128)(2,1)} async-done(((bf16[512,3,1024]{0,1,2:T(4,128)(2,1)}), bf16[512,3,1024]{0,1,2:T(4,128)(2,1)}, u32[]{:S(2)}, u32[]{:S(2)}) %all-to-all-start) | async-done | bytes 3145760 | tf_op jit(solution)/shard_map/all_to_all | solution.py:111
  152.9 6.8 %copy.24 = bf16[4,512,3,256]{1,0,3,2:T(4,128)(2,1)} copy(bf16[4,512,3,256]{1,2,3,0:T(4,128)(2,1)} %bitcast.13) | data formatting | bytes 6291456 | tf_op jit(solution)/shard_map/all_to_all | solution.py:111
  159.7 6.1 reshape.180
  165.8 3.2 slice_bitcast_fusion
  170.8 77.8 %while.12 = (s32[]{:T(128)}, bf16[16,128,4,64]{1,3,2,0:T(8,128)(2,1)}, s32[16]{0:T(128)S(1)}, bf16[2560,4,64]{0,2,1:T(8,128)(2,1)}, bf16[2048,4,64]{0,2,1:T(8,12...) while((s32[]{:T(128)}, ...), condition=%wide.region_6.7_spmd, body=%wide.region_4.6_spmd.sunk | while | flops 85724168 | bytes 4885232 | solution.py:83
  173.6 2.1 fusion.82
  178.4 2.1 fusion.82
  193.0 2.1 fusion.82
  202.7 2.1 fusion.82
  207.6 2.1 fusion.82
  251.7 2.5 copy.26
  254.2 4.3 all-to-all-start.1
  258.5 25.2 %all-to-all-done.1 = bf16[4,512,256]{1,2,0:T(8,128)(2,1)} async-done(((bf16[4,512,256]{1,2,0:T(8,128)(2,1)}), bf16[4,512,256]{1,2,0:T(8,128)(2,1)}, u32[]{:S(2)}, u32[]{:S(2)}) %all-to-all-start.1) | async-done | bytes 1048608 | tf_op jit(solution)/shard_map/all_to_all | solution.py:118
  283.7 2.5 fusion.32
  291.0 3.5 collective-permute-done
  294.5 3.8 collective-permute-done.1
  298.3 2.5 pad_maximum_fusion.5
  300.8 22.5 %gather_fusion = bf16[4096,1024]{1,0:T(8,128)(2,1)} fusion(bf16[768,1024]{1,0:T(8,128)(2,1)} %pad_maximum_fusion.5, s32[4096]{0:T(1024)S(1)} %broadcast_clamp_fusion), kind=kCustom, calls=%fused_computation | custom fusion | bytes 16793600 | tf_op jit(solution)/shard_map/gather | solution.py:125
  323.3 15.4 %reshape.224 = f32[1024,4,1024]{2,1,0:T(4,128)} reshape(bf16[4096,1024]{1,0:T(8,128)(2,1)} %gather_fusion) | data formatting | bytes 25165824 | tf_op jit(solution)/shard_map/convert_element_type | solution.py:125
  338.8 14.7 %reduce_sum.67 = f32[1024,1024]{1,0:T(8,128)} reduce(f32[1024,4,1024]{2,1,0:T(4,128)} %reshape.224, f32[]{:T(128)} %constant.116.clone.1), dimensions={1}, to_apply=%region_7.8 | reduce | flops 3145728 | bytes 20971524 | tf_op jit(solution)/shard_map/reduce_sum | solution.py:125
  353.5 3.7 fusion.47
  357.5 21.9 %all-gather.3.cloned.1.call-done = f32[4096,128]{1,0:T(8,128)} async-done(((f32[1024,128]{1,0:T(8,128)}), f32[4096,128]{1,0:T(8,128)}) %all-gather.3.cloned.1.call-update) | async-done | bytes 2097168 | tf_op jit(solution)/shard_map/all_gather | solution.py:129
  379.4 2.1 multiply_reduce_fusion
  382.9 2.6 fusion.56
  385.5 11.9 %scatter_custom_fusion = f32[768,1024]{1,0:T(8,128)} fusion(s32[1024]{0:T(1024)S(1)} %bitcast.83, f32[1024,1024]{1,0:T(8,128)} %fusion.56, f32[]{:T(128)} %constant.128.clone.1, f32[]{:T(128)} %constant.116.clone.1), kind=kCustom, calls=%fused_computation.35 | custom fusion | flops 2097152 | bytes 7340040 | tf_op jit(solution)/shard_map/scatter-add | solution.py:140
  397.4 13.6 %scatter_custom_fusion.1 = f32[768,1024]{1,0:T(8,128)} fusion(f32[768,1024]{1,0:T(8,128)} %scatter_custom_fusion, s32[1024]{0:T(1024)S(1)} %bitcast.82, f32[1024,1024]{1,0:T(8,128)} %fusion.56, f32[]{:T(128)} %constant.128.clone.1), kind=kCustom, calls=%fused_computation.33 | custom fusion | flops 2097152 | bytes 7340544 | tf_op jit(solution)/shard_map/scatter-add | solution.py:140
  410.9 13.8 %scatter_custom_fusion.2 = f32[768,1024]{1,0:T(8,128)} fusion(f32[768,1024]{1,0:T(8,128)} %scatter_custom_fusion.1, s32[1024]{0:T(1024)S(1)} %bitcast.81, f32[1024,1024]{1,0:T(8,128)} %fusion.56, f32[]{:T(128)} %constant.128.clone.1), kind=kCustom, calls=%fused_computation.31 | custom fusion | flops 2097152 | bytes 7340544 | tf_op jit(solution)/shard_map/scatter-add | solution.py:140
  424.7 13.6 %scatter_custom_fusion.3 = f32[768,1024]{1,0:T(8,128)} fusion(f32[768,1024]{1,0:T(8,128)} %scatter_custom_fusion.2, s32[1024]{0:T(1024)S(1)} %bitcast.80, f32[1024,1024]{1,0:T(8,128)} %fusion.56, f32[]{:T(128)} %constant.128.clone.1), kind=kCustom, calls=%fused_computation.29 | custom fusion | flops 2097152 | bytes 7340544 | tf_op jit(solution)/shard_map/scatter-add | solution.py:140
  438.3 2.3 convert.10
  440.6 3.4 collective-permute-start.2
  445.6 4.4 collective-permute-done.2
  450.0 4.1 collective-permute-done.3
  455.6 3.8 convolution_convert_fusion.1
  459.5 3.7 fusion.46
  463.3 39.2 %reduce-scatter.2.cloned.1.call-done = bf16[256,1024]{1,0:T(8,128)(2,1)} async-done(((bf16[1024,1024]{1,0:T(8,128)(2,1)}), bf16[256,1024]{1,0:T(8,128)(2,1)}) %reduce-scatter.2.cloned.1.call-update) | async-done | bytes 524304 | tf_op jit(solution)/shard_map/reduce_scatter | solution.py:147
  502.5 3.8 fusion.38
  506.4 89.9 %all-reduce.5.cloned.1.call-done = f32[1024,128]{1,0:T(8,128)} async-done(((f32[1024,128]{1,0:T(8,128)}), f32[1024,128]{1,0:T(8,128)}) %all-reduce.5.cloned.1.call-update) | async-done | bytes 524304 | tf_op jit(solution)/shard_map/psum | solution.py:133
  598.2 34.1 %all-reduce.3.cloned.1.call-done = bf16[256,1024]{1,0:T(8,128)(2,1)} async-done(((bf16[256,1024]{1,0:T(8,128)(2,1)}), bf16[256,1024]{1,0:T(8,128)(2,1)}) %all-reduce.3.cloned.1.call-update) | async-done | bytes 524304 | tf_op jit(solution)/shard_map/psum | solution.py:155
  632.3 2.1 convert_multiply_fusion
  (136 shorter events, 86.6 us)
Async XLA Ops:
  7.2 276.5 %copy-start = (bf16[1024,1024]{1,0:T(8,128)(2,1)S(1)}, bf16[1024,1024]{1,0:T(8,128)(2,1)}, u32[]{:S(2)}) copy-start(bf16[1024,1024]{1,0:T(8,128)(2,1)} %param.15) | copy-start | bytes 6291460
  16.5 4.1 copy-start.2
  53.0 99.9 %all-to-all-start = ((bf16[512,3,1024]{0,1,2:T(4,128)(2,1)}), bf16[512,3,1024]{0,1,2:T(4,128)(2,1)}, u32[]{:S(2)}, u32[]{:S(2)}) async-start(bf16[512,3,1024]{0,1,2:T(4,128)(2,1)} %copy.23), calls=%async_computation | async-start | bytes 8388608 | tf_op jit(solution)/shard_map/all_to_all | solution.py:111
  251.7 32.0 %copy-start.4 = (bf16[1,512,1024]{2,1,0:T(8,128)(2,1)S(1)}, bf16[1,512,1024]{2,1,0:T(8,128)(2,1)}, u32[]{:S(2)}) copy-start(bf16[1,512,1024]{2,1,0:T(8,128)(2,1)} %param.13) | copy-start | bytes 3145732
  254.2 29.5 %all-to-all-start.1 = ((bf16[4,512,256]{1,2,0:T(8,128)(2,1)}), bf16[4,512,256]{1,2,0:T(8,128)(2,1)}, u32[]{:S(2)}, u32[]{:S(2)}) async-start(bf16[4,512,256]{1,2,0:T(8,128)(2,1)} %copy.26), calls=%async_computation.1 | async-start | bytes 2097152 | tf_op jit(solution)/shard_map/all_to_all | solution.py:118
  258.4 121.0 %all-gather.3.cloned.1.call-start = ((), (), s32[]{:S(2)}) async-start(), calls=%async_computation.6 | async-start | bytes 2621440 | tf_op jit(solution)/shard_map/all_gather | solution.py:129
  283.7 6.8 %copy-start.8 = (s32[1024,4]{0,1:T(4,128)S(1)}, s32[1024,4]{0,1:T(4,128)}, u32[]{:S(2)}) copy-start(s32[1024,4]{0,1:T(4,128)} %param.17) | copy-start | bytes 49156
  286.2 1.0 copy-start.6
  287.9 6.6 %collective-permute-start = (bf16[128,1024]{1,0:T(8,128)(2,1)}, bf16[128,1024]{1,0:T(8,128)(2,1)S(1)}, u32[]{:S(2)}, u32[]{:S(2)}) collective-permute-start(bf16[128,1024]{1,0:T(8,128)(2,1)} %get-tuple-element.85), channel_id=1, source_target_pairs={{0,4},{4,8},{8,12},{1,5},{5,9},{9,13},{2,6},{6,10},{10,14},{3,7},{... | collective-permute-start | bytes 786440 | tf_op jit(solution)/shard_map/ppermute | solution.py:24
  289.2 9.2 %collective-permute-start.1 = (bf16[128,1024]{1,0:T(8,128)(2,1)S(1)}, bf16[128,1024]{1,0:T(8,128)(2,1)S(1)}, u32[]{:S(2)}, u32[]{:S(2)}) collective-permute-start(bf16[128,1024]{1,0:T(8,128)(2,1)S(1)} %get-tuple-element.86), channel_id=1, source_target_pairs={{4,0},{8,4},{12,8},{5,1},{9,5},{13,9},{6,2},{10,6},{14,10},{7,3},{... | collective-permute-start | bytes 786440 | tf_op jit(solution)/shard_map/ppermute | solution.py:26
  338.8 14.7 %copy-start.7 = (bf16[1024,128]{1,0:T(8,128)(2,1)S(1)}, bf16[1024,128]{1,0:T(8,128)(2,1)}, u32[]{:S(2)}) copy-start(bf16[1024,128]{1,0:T(8,128)(2,1)} %param.16) | copy-start | bytes 786436
  357.2 24.4 %copy-start.3 = (f32[1024,128]{1,0:T(8,128)S(1)}, f32[1024,128]{1,0:T(8,128)}, u32[]{:S(2)}) copy-start(f32[1024,128]{1,0:T(8,128)} %fusion.47) | copy-start | bytes 1572868
  357.2 24.4 %copy-start.9 = (f32[1024]{0:T(1024)S(1)}, f32[1024]{0:T(1024)}, u32[]{:S(2)}) copy-start(f32[1024]{0:T(1024)} %param.19) | copy-start | bytes 12292
  357.2 145.3 %reduce-scatter.2.cloned.1.call-start = ((), (), s32[]{:S(2)}) async-start(), calls=%async_computation.3 | async-start | bytes 2621440 | tf_op jit(solution)/shard_map/reduce_scatter | solution.py:147
  438.3 7.0 %copy-start.1 = (f32[768,1024]{1,0:T(8,128)S(1)}, f32[768,1024]{1,0:T(8,128)}, u32[]{:S(2)}) copy-start(f32[768,1024]{1,0:T(8,128)} %scatter_custom_fusion.3) | copy-start | bytes 9437188
  440.6 9.3 %collective-permute-start.2 = (bf16[128,1024]{1,0:T(8,128)(2,1)S(1)}, bf16[128,1024]{1,0:T(8,128)(2,1)S(1)}, u32[]{:S(2)}, u32[]{:S(2)}) collective-permute-start(bf16[128,1024]{1,0:T(8,128)(2,1)S(1)} %get-tuple-element.83), channel_id=1, source_target_pairs={{0,4},{4,8},{8,12},{1,5},{5,9},{9,13},{2,6},{6,10},{10,14},{3,7},{... | collective-permute-start | bytes 786440 | tf_op jit(solution)/shard_map/ppermute | solution.py:24
  444.0 10.1 %collective-permute-start.3 = (bf16[128,1024]{1,0:T(8,128)(2,1)S(1)}, bf16[128,1024]{1,0:T(8,128)(2,1)S(1)}, u32[]{:S(2)}, u32[]{:S(2)}) collective-permute-start(bf16[128,1024]{1,0:T(8,128)(2,1)S(1)} %get-tuple-element.84), channel_id=1, source_target_pairs={{4,0},{8,4},{12,8},{5,1},{9,5},{13,9},{6,2},{10,6},{14,10},{7,3},{... | collective-permute-start | bytes 786440 | tf_op jit(solution)/shard_map/ppermute | solution.py:26
  454.3 1.4 copy-start.5
  459.4 136.9 %all-reduce.5.cloned.1.call-start = ((), (), s32[]{:S(2)}) async-start(), calls=%async_computation.5 | async-start | bytes 1048576 | tf_op jit(solution)/shard_map/psum | solution.py:133
  463.2 169.1 %all-reduce.3.cloned.1.call-start = ((), (), s32[]{:S(2)}) async-start(), calls=%async_computation.4 | async-start | bytes 1048576 | tf_op jit(solution)/shard_map/psum | solution.py:155
Sparse Core Ops, SparseCore 0:
  357.3 22.0 all-gather.2
  459.6 42.9 reduce-scatter.1
  506.9 89.3 all-reduce.4
  598.7 33.6 all-reduce.2
where the time goes:
time: 649 us; the launch traced here: 641 us
  waiting for transfers between devices  320 us (49%)
  other arithmetic  98.6 us (15%)
  local copies, waits for them, and re-layouts  96.6 us (15%)
  matrix products  83.3 us (13%)
  starting transfers between devices  18.4 us (3%)
  between operations  14.5 us (2%)
  loops' own time  10.5 us (2%)
    all_to_all x1, waiting for transfers between devices, body(): lax.all_to_all(stacked, 'seq', split_axis=2, concat_axis=0, tiled=True)  93.4 us
    psum x1, waiting for transfers between devices, body(): lax.psum(decoder_term, ('seq', 'member')) / math.sqrt(members * grid_total)  89.9 us
    scatter-add x4, other arithmetic, body(): wide_cotangent = wide_cotangent.at[local[:, column]].add(share)  52.8 us
    reduce_scatter x1, waiting for transfers between devices, body(): lax.psum_scatter(jnp.dot(attended.T, latent_cotangent, preferred_element_...  39.2 us
    psum x1, waiting for transfers between devices, body(): shard = lax.psum(shard.astype(jnp.bfloat16), 'member').astype(jnp.float32)  34.1 us
    dot_general x16, matrix products, one_block(): jnp.einsum('hqk,khe->qhe', shares, value_block, preferred_element_type=jn...  33.5 us
    all_to_all x1, waiting for transfers between devices, body(): lax.all_to_all(head_result, 'seq', split_axis=0, concat_axis=1, tiled=True)  25.2 us
    dot_general x16, matrix products, one_block(): jnp.einsum('qhe,khe->hqk', query_block, key_block, preferred_element_type...  23.5 us
  transfers between devices with their start and end apart: 10, of which 10 were waited for; matrix products, arithmetic and copies ran while one was open for 2% of the time, Pallas kernels for 0%

commit v1 on v0

v1 whole, which is shorter than its diff:
```python
import functools
import math

import jax
import jax.numpy as jnp
from jax import lax
from jax.experimental import pallas as pl
from jax.experimental.pallas import tpu as pltpu
from jax.sharding import PartitionSpec as P

HEAD_DIM = 64
WINDOW = 512
REACH = 128
LANES = 128
COLS = 512

smooth = 0.1
f32 = jnp.float32
bf16 = jnp.bfloat16


def from_sides(cells, width):
    count = lax.axis_size("seq")
    rows = cells.shape[0]
    right = [(i, i + 1) for i in range(count - 1)]
    left = [(i + 1, i) for i in range(count - 1)]
    return (
        lax.ppermute(cells[rows - width :], "seq", right),
        lax.ppermute(cells[:width], "seq", left),
    )


def normalize(rows):
    values = rows.astype(f32)
    centre = jnp.mean(values, axis=-1, keepdims=True)
    values = values - centre
    spread = jnp.mean(values * values, axis=-1, keepdims=True)
    return (values * lax.rsqrt(spread + 1e-05)).astype(bf16)


def project_kernel(first, width, *refs):
    parts, weight, out, normed = refs[:-3], refs[-3], refs[-2], refs[-1]
    step = pl.program_id(0) + first

    @pl.when(pl.program_id(0) == 0)
    def _():
        row = 0
        for part in parts:
            normed[row : row + part.shape[0], :] = normalize(part[...])
            row += part.shape[0]

    mixed = jnp.dot(normed[...], weight[...], preferred_element_type=f32)
    columns = mixed.shape[1]

    @pl.when(step * columns >= 2 * width)
    def _():
        out[...] = mixed.astype(bf16)

    @pl.when(step * columns < 2 * width)
    def _():
        side = 256
        down = lax.broadcasted_iota(jnp.int32, (side, side), 0) >> 6
        across = lax.broadcasted_iota(jnp.int32, (side, side), 1) >> 6
        same = jnp.where(down == across, 1.0 / HEAD_DIM, 0.0).astype(bf16)
        scale = jnp.where(step * columns < width, HEAD_DIM**-0.5, 1.0)
        for at in range(0, columns, side):
            piece = mixed[:, at : at + side]
            mean = jnp.dot((piece * piece).astype(bf16), same, preferred_element_type=f32)
            out[:, at : at + side] = (piece * (lax.rsqrt(mean + 1e-06) * scale)).astype(bf16)


def project(parts, weight, first):
    width = weight.shape[0]
    rows = sum(part.shape[0] for part in parts)
    steps = weight.shape[1] // COLS - first
    return pl.pallas_call(
        functools.partial(project_kernel, first, width),
        grid=(steps,),
        in_specs=[pl.BlockSpec(part.shape, lambda j: (0, 0)) for part in parts]
        + [pl.BlockSpec((width, COLS), lambda j: (0, j + first))],
        out_specs=pl.BlockSpec((rows, COLS), lambda j: (0, j)),
        out_shape=jax.ShapeDtypeStruct((rows, steps * COLS), bf16),
        scratch_shapes=[pltpu.VMEM((rows, width), bf16)],
        compiler_params=pltpu.CompilerParams(vmem_limit_bytes=32 << 20),
        cost_estimate=pl.CostEstimate(
            flops=2 * rows * width * steps * COLS,
            bytes_accessed=2 * (width * steps * COLS + rows * width + rows * steps * COLS),
            transcendentals=0,
        ),
    )(*parts, weight)


def attend_kernel(
    ends, query, key_own, key_side, value_own, value_side, tokens, decoder, joint,
    out, mapped, keys, values,
):
    half = WINDOW // 2
    rows = query.shape[0]

    @pl.when(pl.program_id(0) == 0)
    def _():
        mapped[...] = jnp.dot(tokens[...], decoder[...], preferred_element_type=f32)

    keys[:half, :] = key_side[:half, :]
    keys[half : half + rows, :] = key_own[...]
    keys[half + rows :, :] = key_side[half:, :]
    first = lax.broadcasted_iota(jnp.int32, (1, LANES), 1) < HEAD_DIM
    chunks = (
        (0, value_side[:half, :], ends[0].astype(f32)),
        (half, value_own[...], 1.0),
        (half + rows, value_side[half:, :], ends[1].astype(f32)),
    )
    for at, part, exists in chunks:
        ones = jnp.full(part.shape, exists, f32).astype(bf16)
        values[0, at : at + part.shape[0], :] = jnp.where(first, part, ones)
        values[1, at : at + part.shape[0], :] = jnp.where(first, ones, part)
    block = half
    down = lax.broadcasted_iota(jnp.int32, (block, block), 0)
    across = lax.broadcasted_iota(jnp.int32, (block, block), 1)
    span = block + WINDOW
    for start in range(0, rows, block):
        own = query[start : start + block, :]
        here = keys[start : start + span, :]
        sums = []
        for head in range(2):
            part = jnp.where(first == (head == 0), own, jnp.zeros_like(own))
            scores = lax.dot_general(
                part, here, (((1,), (1,)), ((), ())), preferred_element_type=f32
            )
            weights = jnp.exp(scores)
            weights = jnp.concatenate(
                [
                    jnp.where(across >= down, weights[:, :block], 0.0).astype(bf16),
                    weights[:, block : span - block].astype(bf16),
                    jnp.where(across < down, weights[:, span - block :], 0.0).astype(bf16),
                ],
                axis=1,
            )
            total = jnp.dot(
                weights, values[head, start : start + span, :], preferred_element_type=f32
            )
            sums.append(total / pltpu.roll(total, HEAD_DIM, 1))
        result = jnp.where(first, sums[0], sums[1]).astype(bf16)
        out[start : start + block, :] = result
        mapped[start : start + block, :] += jnp.dot(
            result, joint[...], preferred_element_type=f32
        )


def attend(ends, own, side, tokens, decoder, joint):
    rows, width = tokens.shape
    steps = width // LANES
    fields = decoder.shape[1]
    wide = rows + WINDOW

    def column(array, offset):
        return pl.BlockSpec((array.shape[0], LANES), lambda j: (0, j + offset))

    return pl.pallas_call(
        attend_kernel,
        grid=(steps,),
        in_specs=[
            pl.BlockSpec(memory_space=pltpu.SMEM),
            column(own, 0),
            column(own, steps),
            column(side, 0),
            column(own, 2 * steps),
            column(side, steps),
            pl.BlockSpec(tokens.shape, lambda j: (0, 0)),
            pl.BlockSpec(decoder.shape, lambda j: (0, 0)),
            pl.BlockSpec((LANES, fields), lambda j: (j, 0)),
        ],
        out_specs=[
            pl.BlockSpec((rows, LANES), lambda j: (0, j)),
            pl.BlockSpec((rows, fields), lambda j: (0, 0)),
        ],
        out_shape=[
            jax.ShapeDtypeStruct((rows, width), bf16),
            jax.ShapeDtypeStruct((rows, fields), f32),
        ],
        scratch_shapes=[pltpu.VMEM((wide, LANES), bf16), pltpu.VMEM((2, wide, LANES), bf16)],
        compiler_params=pltpu.CompilerParams(vmem_limit_bytes=32 << 20),
    )(ends, own, own, side, own, side, tokens, decoder, joint)


def slope(diff):
    return diff * lax.rsqrt(diff * diff + smooth * smooth)


def body(tokens, input_weight, output_weight, decoder_weight, neighbours, observed, cell_area):
    own_tokens = tokens[0]
    tok_rows, width = own_tokens.shape
    fields_count = decoder_weight.shape[1]
    seq_count = lax.axis_size("seq")
    members = lax.axis_size("member")
    seq_place = lax.axis_index("seq")
    fan_count = neighbours.shape[1]
    grid_rows = neighbours.shape[0]
    wide_rows = tok_rows + 2 * REACH

    before, after = from_sides(own_tokens, WINDOW // 2)
    own = project([own_tokens], input_weight, 0)
    joint = jnp.dot(output_weight, decoder_weight, preferred_element_type=f32).astype(bf16)
    local = neighbours - (seq_place * tok_rows - REACH)
    places = jnp.arange(wide_rows, dtype=jnp.int32)
    counts = jnp.zeros((grid_rows, wide_rows), f32)
    for column in range(fan_count):
        counts = counts + (local[:, column][:, None] == places[None, :]).astype(f32)
    counts = (counts / fan_count).astype(bf16)
    side = project([before, after], input_weight, width // COLS)
    ends = jnp.stack([seq_place > 0, seq_place < seq_count - 1]).astype(jnp.int32)
    attended, mapped = attend(ends, own, side, own_tokens, decoder_weight, joint)

    mapped = mapped.astype(bf16)
    before, after = from_sides(mapped, REACH)
    mapped = jnp.concatenate([before, mapped, after], axis=0)
    every = lax.all_gather(mapped, "member", axis=0, tiled=False)
    all_fields = jnp.einsum("gt,mtf->mgf", counts, every, preferred_element_type=f32)
    fields = lax.dynamic_index_in_dim(all_fields, lax.axis_index("member"), 0, keepdims=False)
    pairs = jnp.sum(slope(fields[None] - all_fields), axis=0)
    single = slope(fields - observed)
    cotangent = (
        cell_area[:, None] * (single / members - pairs / (members * (members - 1)))
    ).astype(bf16)
    spread = lax.dot_general(
        counts, cotangent, (((0,), (0,)), ((), ())), preferred_element_type=f32
    )
    edges = jnp.concatenate([spread[:REACH], spread[REACH + tok_rows :]], axis=0)
    before, after = from_sides(edges, REACH)
    middle = spread[REACH : REACH + tok_rows]
    middle = middle.at[:REACH].add(before).at[tok_rows - REACH :].add(after).astype(bf16)
    attention_cotangent = lax.dot_general(
        middle, joint, (((1,), (1,)), ((), ())), preferred_element_type=f32
    ).astype(bf16)
    output_term = lax.dot_general(
        attended, middle, (((0,), (0,)), ((), ())), preferred_element_type=f32
    )
    decoder_term = lax.dot_general(
        own_tokens, middle, (((0,), (0,)), ((), ())), preferred_element_type=f32
    ) + lax.dot_general(
        output_weight, output_term.astype(bf16), (((0,), (0,)), ((), ())),
        preferred_element_type=f32,
    )
    both = lax.psum(
        jnp.concatenate([output_term, decoder_term], axis=1), ("seq", "member")
    )
    decoder_gradient = both[:, fields_count:] / math.sqrt(members * grid_rows * seq_count)
    rows = width // seq_count
    output_rows = lax.dynamic_slice_in_dim(both[:, :fields_count], seq_place * rows, rows, 0)
    output_gradient = lax.dot_general(
        output_rows.astype(bf16), decoder_weight, (((1,), (1,)), ((), ())),
        preferred_element_type=f32,
    ) / math.sqrt(members * tok_rows * seq_count)
    return (attention_cotangent[None], output_gradient, decoder_gradient)


def solution(mesh):
    in_specs = (
        P(("group", "member"), "seq", None),
        P(),
        P(),
        P(),
        P("seq", None),
        P(("group", "seq"), None),
        P("seq"),
    )
    out_specs = (P(("group", "member"), "seq", None), P(("group", "seq"), None), P("group", None))
    return jax.shard_map(body, mesh=mesh, in_specs=in_specs, out_specs=out_specs, check_vma=False)
```

time: 649 us -> 194 us (0.30); the launches traced: 641 us -> 194 us
  waiting for transfers between devices: 320 us -> 99.6 us
  other arithmetic: 98.6 us -> 3.44 us
  local copies, waits for them, and re-layouts: 96.6 us -> 11.6 us
  matrix products: 83.3 us -> 12.5 us
  Pallas kernels: 0 us -> 27.8 us
  loops' own time: 10.5 us -> 0 us
  blocking collectives: 0 us -> 8.58 us
    all_to_all x2 -> x0, waiting for transfers between devices: 119 us -> none  [the longest x1 93.4 us: body(): lax.all_to_all(stacked, 'seq', split_axis=2, concat_axis=0, tiled=True)]
    dot_general x39 -> x8, matrix products: 83.3 us -> 12.5 us  [the longest x1 4.12 us: body(): jnp.einsum('gt,mtf->mgf', counts, every, preferred_element_type=f32)]
    scatter-add x6 -> x2, other arithmetic: 53 us -> 0.02 us  [body(): middle.at[:REACH].add(before).at[tok_rows - REACH:].add(after).astype(bf16)]
    reduce_scatter x1 -> x0, waiting for transfers between devices: 39.2 us -> none  [body(): lax.psum_scatter(jnp.dot(attended.T, latent_cotangent, preferred_element_...]
    psum x2 -> x1, waiting for transfers between devices: 124 us -> 90 us  [body(): lax.psum(jnp.concatenate([output_term, decoder_term], axis=1), ('seq', 'm...]
    pallas_call x0 -> x3, Pallas kernels: none -> 27.8 us  [the longest x1 14.9 us: attend(): pl.pallas_call(attend_kernel, grid=(steps,), in_specs=[pl.BlockSpec(memor...]
    reduce_sum x6 -> x1, other arithmetic: 23.8 us -> 0.42 us  [body(): pairs = jnp.sum(slope(fields[None] - all_fields), axis=0)]
    gather x1 -> x0, local copies, waits for them, and re-layouts: 22.5 us -> none  [body(): latent_wide[local].astype(jnp.float32)]
  transfers between devices with their start and end apart: 10 -> 7, of which waited for: 10 -> 5; matrix products, arithmetic and copies ran while one was open for 2% -> 3% of each run, Pallas kernels for 0% -> 4%
where the time goes in v1:
time: 194 us
  waiting for transfers between devices  99.6 us (51%)
  Pallas kernels  27.8 us (14%)
  starting transfers between devices  15.8 us (8%)
  between operations  14.4 us (7%)
  matrix products  12.5 us (6%)
  local copies, waits for them, and re-layouts  11.6 us (6%)
  blocking collectives  8.58 us (4%)
  other arithmetic  3.44 us (2%)
    psum x1, waiting for transfers between devices, body(): lax.psum(jnp.concatenate([output_term, decoder_term], axis=1), ('seq', 'm...  90 us
    pallas_call x1, Pallas kernels, attend(): pl.pallas_call(attend_kernel, grid=(steps,), in_specs=[pl.BlockSpec(memor...  14.9 us
    pallas_call x2, Pallas kernels, project(): pl.pallas_call(functools.partial(project_kernel, first, width), grid=(ste...  12.9 us
    ppermute x3, starting transfers between devices, from_sides(): lax.ppermute(cells[rows - width:], 'seq', right)  11.9 us
    ppermute x3, waiting for transfers between devices, from_sides(): lax.ppermute(cells[:width], 'seq', left)  9.02 us
    all_gather x1, blocking collectives, body(): every = lax.all_gather(mapped, 'member', axis=0, tiled=False)  8.58 us
    unnamed x28, local copies, waits for them, and re-layouts  7.43 us
    dot_general x1, matrix products, body(): jnp.einsum('gt,mtf->mgf', counts, every, preferred_element_type=f32)  4.12 us
  transfers between devices with their start and end apart: 7, of which 5 were waited for; matrix products, arithmetic and copies ran while one was open for 3% of the time, Pallas kernels for 4%

profile of v1, /device:TPU:0, one launch (start us, length us, event | category | flops | bytes accessed | tf_op | source)
XLA Modules:
  0.0 193.6 jit_solution(13920844536067212029)
XLA Ops:
  7.2 0.0 copy-start
  7.2 0.0 all-reduce.2.cloned.1.call-start
  7.2 2.4 %slice_bitcast_fusion = (bf16[256,1024]{1,0:T(8,128)(2,1)}, bf16[256,1024]{1,0:T(8,128)(2,1)}) fusion(bf16[1,512,1024]{2,1,0:T(8,128)(2,1)} %param.11), kind=kLoop, calls=%fused_computation.20 | loop fusion | bytes 2097152 | tf_op jit(solution)/shard_map/slice | solution.py:29
  9.6 5.7 %collective-permute-start = (bf16[256,1024]{1,0:T(8,128)(2,1)}, bf16[256,1024]{1,0:T(8,128)(2,1)}, u32[]{:S(2)}, u32[]{:S(2)}) collective-permute-start(bf16[256,1024]{1,0:T(8,128)(2,1)} %get-tuple-element.35), channel_id=1, source_target_pairs={{0,4},{4,8},{8,12},{1,5},{5,9},{9,13},{2,6},{6,10},{10,14},{3,7},{... | collective-permute-start | bytes 1572872 | tf_op jit(solution)/shard_map/ppermute | solution.py:28
  15.4 1.3 collective-permute-start.1
  16.7 0.1 add_convert_fusion.ends
  16.7 2.4 %convolution_convert_fusion.1.joint = bf16[1024,128]{1,0:T(8,128)(2,1)} fusion(bf16[1024,1024]{1,0:T(8,128)(2,1)S(1)} %copy-done, bf16[1024,128]{1,0:T(8,128)(2,1)} %decoder.1), kind=kOutput, calls=%fused_computation.15 | convolution fusion | flops 268566528 | bytes 2621440 | tf_op jit(solution)/shard_map/dot_general | solution.py:203
  19.1 0.0 copy-start.2
  19.1 2.8 %copy-done.2 = bf16[1024,3072]{1,0:T(8,128)(2,1)S(1)} copy-done((bf16[1024,3072]{1,0:T(8,128)(2,1)S(1)}, bf16[1024,3072]{1,0:T(8,128)(2,1)}, u32[]{:S(2)}) %copy-start.2) | copy-done | bytes 6291480
  21.9 7.0 %shard_map.94.query.key_own.value_own = bf16[512,3072]{1,0:T(8,128)(2,1)S(1)} custom-call(bf16[512,1024]{1,0:T(8,128)(2,1)S(1)} %bitcast.36, bf16[1024,3072]{1,0:T(8,128)(2,1)S(1)} %copy-done.2), custom_call_target="tpu_custom_call" | custom-call | flops 3221225472 | bytes 10485760 | tf_op jit(solution)/shard_map/pallas_call | solution.py:76
  28.9 0.0 copy-start.3
  28.9 0.0 copy-start.4
  29.0 2.0 %collective-permute-done.1.refs_1_ = bf16[256,1024]{1,0:T(8,128)(2,1)} collective-permute-done((bf16[256,1024]{1,0:T(8,128)(2,1)}, bf16[256,1024]{1,0:T(8,128)(2,1)}, u32[]{:S(2)}, u32[]{:S(2)}) %collective-permute-start.1) | collective-permute-done | bytes 524320 | tf_op jit(solution)/shard_map/ppermute | solution.py:29
  30.9 5.9 %shard_map.95.key_side.value_side = bf16[512,2048]{1,0:T(8,128)(2,1)S(1)} custom-call(bf16[256,1024]{1,0:T(8,128)(2,1)} %collective-permute-done.refs_0_, bf16[256,1024]{1,0:T(8,128)(2,1)} %collective-permute-done.1.refs_1_, bf16[1024,3072]{1,0:T(8,128)(2,1)S(1)} %copy-done.2), custom_call_target="tpu_custom_call" | custom-call | flops 2147483648 | bytes 7340032 | tf_op jit(solution)/shard_map/pallas_call | solution.py:76
  36.8 14.9 %shard_map.96 = (bf16[512,1024]{1,0:T(8,128)(2,1)S(1)}, f32[512,128]{1,0:T(8,128)S(1)}) custom-call(s32[2]{0:T(128)S(1)} %add_convert_fusion.ends, bf16[512,3072]{1,0:T(8,128)(2,1)S(1)} %shard_map.94.query.key_own.value_own, bf16[512,3072]{1,0:T(8,128)(2,1)S(1)} %shard_map.94.query.key_own.value_own, bf16[512,2048]{1,0:T(8,128)(2,1)S(1)} %shard_map.95.key_side.value_side, ...), custom_call_target="tpu_custom_call" | custom-call | tf_op jit(solution)/shard_map/pallas_call | solution.py:159
  51.7 0.0 copy-start.6
  51.7 1.0 copy-done.6
  52.7 0.6 fusion.24
  53.4 3.3 %collective-permute-start.2 = (bf16[128,128]{1,0:T(8,128)(2,1)}, bf16[128,128]{1,0:T(8,128)(2,1)}, u32[]{:S(2)}, u32[]{:S(2)}) collective-permute-start(bf16[128,128]{1,0:T(8,128)(2,1)} %get-tuple-element.38), channel_id=1, source_target_pairs={{0,4},{4,8},{8,12},{1,5},{5,9},{9,13},{2,6},{6,10},{10,14},{3,7},{... | collective-permute-start | bytes 98312 | tf_op jit(solution)/shard_map/ppermute | solution.py:28
  56.7 1.3 collective-permute-start.3
  58.0 2.0 %copy.11 = f32[1024,128]{0,1:T(8,128)} copy(f32[1024,128]{1,0:T(8,128)} %param.16) | data formatting | bytes 1048576 | tf_op args[5]
  60.0 2.8 %collective-permute-done.3 = bf16[128,128]{1,0:T(8,128)(2,1)} collective-permute-done((bf16[128,128]{1,0:T(8,128)(2,1)}, bf16[128,128]{1,0:T(8,128)(2,1)}, u32[]{:S(2)}, u32[]{:S(2)}) %collective-permute-start.3) | collective-permute-done | bytes 32800 | tf_op jit(solution)/shard_map/ppermute | solution.py:29
  62.8 0.8 pad_maximum_fusion.1
  63.6 8.6 %all-gather = bf16[3072,128]{1,0:T(8,128)(2,1)S(1)} all-gather(bf16[768,128]{1,0:T(8,128)(2,1)S(1)} %pad_maximum_fusion.1), channel_id=2, replica_groups=mesh['group'=2,'seq'=4,'member'=4] {'member'}, dimensions={0}, use_global_device_ids=true | all-gather | bytes 983040 | tf_op jit(solution)/shard_map/all_gather | solution.py:217
  72.1 4.1 %fusion = f32[4,128,1024]{2,1,0:T(8,128)S(1)} fusion(bf16[4,768,128]{2,1,0:T(8,128)(2,1)S(1)} %bitcast.38, s32[1024]{0:T(1024)S(1)} %bitcast.41, s32[1024]{0:T(1024)S(1)} %bitcast.43, s32[1024]{0:T(1024)S(1)} %bitcast.45, s32[1024]{0:T(1024)S(1)} %bitcast.39), kind=kOutput, calls=%fused_computation.7 | convolution fusion | flops 815529984 | bytes 2899968 | tf_op jit(solution)/shard_map/gt,mtf->mgf/dot_general | solution.py:218
  76.3 0.0 copy-start.12
  76.3 0.1 dynamic-slice_bitcast_fusion
  76.3 0.4 multiply_reduce_fusion
  76.8 0.5 copy-done.10
  77.3 2.1 %fusion.2 = f32[768,128]{1,0:T(8,128)S(1)} fusion(s32[1024]{0:T(1024)S(1)} %bitcast.42, s32[1024]{0:T(1024)S(1)} %bitcast.44, s32[1024]{0:T(1024)S(1)} %bitcast.46, s32[1024]{0:T(1024)S(1)} %bitcast.40, f32[1024,128]{0,1:T(8,128)S(1)} %multiply_reduce_fusion, f32[1024,128]{0,1:T(8,128)S(1)} %dynamic-slice_bitcast_fusion, f32[1024,128]{0,1:T(8,128)S(1)} %copy-done.10, ...), kind=kOutput, calls=%fused_computation.10 | convolution fusion | flops 212729856 | bytes 1986560 | tf_op jit(solution)/shard_map/dot_general | solution.py:225
  79.5 2.9 %collective-permute-start.4 = (f32[128,128]{1,0:T(8,128)S(1)}, f32[128,128]{1,0:T(8,128)S(1)}, u32[]{:S(2)}, u32[]{:S(2)}) collective-permute-start(f32[128,128]{1,0:T(8,128)S(1)} %get-tuple-element.37), channel_id=1, source_target_pairs={{0,4},{4,8},{8,12},{1,5},{5,9},{9,13},{2,6},{6,10},{10,14},{3,7},{... | collective-permute-start | bytes 196616 | tf_op jit(solution)/shard_map/ppermute | solution.py:28
  82.4 1.3 collective-permute-start.5
  83.7 0.6 collective-permute-done.4
  84.3 4.3 %collective-permute-done.5 = f32[128,128]{1,0:T(8,128)S(1)} collective-permute-done((f32[128,128]{1,0:T(8,128)S(1)}, f32[128,128]{1,0:T(8,128)S(1)}, u32[]{:S(2)}, u32[]{:S(2)}) %collective-permute-start.5) | collective-permute-done | bytes 65568 | tf_op jit(solution)/shard_map/ppermute | solution.py:29
  88.6 0.0 copy-start.8
  88.6 0.4 fusion.16
  89.0 0.4 fusion.5
  89.4 0.3 fusion.4
  89.8 0.0 copy-start.5
  89.8 1.0 pad_maximum_fusion
  90.8 0.0 all-reduce.2.cloned.1.call-update
  90.9 0.1 copy-done.9
  90.9 1.4 fusion.3
  92.3 90.0 %all-reduce.2.cloned.1.call-done = f32[1024,256]{0,1:T(8,128)} async-done(((f32[1024,256]{0,1:T(8,128)}), f32[1024,256]{0,1:T(8,128)}) %all-reduce.2.cloned.1.call-update) | async-done | bytes 1048592 | tf_op jit(solution)/shard_map/psum | solution.py:244
  182.3 1.1 slice_multiply_fusion
  183.4 1.0 copy.12
  184.4 1.1 slice.112
  185.5 1.3 convolution_multiply_fusion
  (23 shorter events, 0.1 us)
Async XLA Ops:
  7.2 9.6 %copy-start = (bf16[1024,1024]{1,0:T(8,128)(2,1)S(1)}, bf16[1024,1024]{1,0:T(8,128)(2,1)}, u32[]{:S(2)}) copy-start(bf16[1024,1024]{1,0:T(8,128)(2,1)} %param.13) | copy-start | bytes 6291460
  7.2 11.9 %copy-start.1 = (bf16[1,512,1024]{2,1,0:T(8,128)(2,1)S(1)}, bf16[1,512,1024]{2,1,0:T(8,128)(2,1)}, u32[]{:S(2)}) copy-start(bf16[1,512,1024]{2,1,0:T(8,128)(2,1)} %param.11) | copy-start | bytes 3145732
  7.2 11.9 %copy-start.11 = (s32[1024,4]{0,1:T(4,128)S(1)}, s32[1024,4]{0,1:T(4,128)}, u32[]{:S(2)}) copy-start(s32[1024,4]{0,1:T(4,128)} %param.15) | copy-start | bytes 49156
  7.2 175.1 %all-reduce.2.cloned.1.call-start = ((), (), s32[]{:S(2)}) async-start(), calls=%async_computation | async-start | bytes 2097152 | tf_op jit(solution)/shard_map/psum | solution.py:244
  9.6 19.3 %collective-permute-start = (bf16[256,1024]{1,0:T(8,128)(2,1)}, bf16[256,1024]{1,0:T(8,128)(2,1)}, u32[]{:S(2)}, u32[]{:S(2)}) collective-permute-start(bf16[256,1024]{1,0:T(8,128)(2,1)} %get-tuple-element.35), channel_id=1, source_target_pairs={{0,4},{4,8},{8,12},{1,5},{5,9},{9,13},{2,6},{6,10},{10,14},{3,7},{... | collective-permute-start | bytes 1572872 | tf_op jit(solution)/shard_map/ppermute | solution.py:28
  15.4 15.6 %collective-permute-start.1 = (bf16[256,1024]{1,0:T(8,128)(2,1)}, bf16[256,1024]{1,0:T(8,128)(2,1)}, u32[]{:S(2)}, u32[]{:S(2)}) collective-permute-start(bf16[256,1024]{1,0:T(8,128)(2,1)} %get-tuple-element.34), channel_id=1, source_target_pairs={{4,0},{8,4},{12,8},{5,1},{9,5},{13,9},{6,2},{10,6},{14,10},{7,3},{... | collective-permute-start | bytes 1572872 | tf_op jit(solution)/shard_map/ppermute | solution.py:29
  19.1 2.8 %copy-start.2 = (bf16[1024,3072]{1,0:T(8,128)(2,1)S(1)}, bf16[1024,3072]{1,0:T(8,128)(2,1)}, u32[]{:S(2)}) copy-start(bf16[1024,3072]{1,0:T(8,128)(2,1)} %refs_2_.1) | copy-start | bytes 18874372
  28.9 7.9 %copy-start.3 = (bf16[1024,128]{1,0:T(8,128)(2,1)S(1)}, bf16[1024,128]{1,0:T(8,128)(2,1)}, u32[]{:S(2)}) copy-start(bf16[1024,128]{1,0:T(8,128)(2,1)} %decoder.1) | copy-start | bytes 786436
  28.9 7.9 %copy-start.4 = (bf16[1024,128]{1,0:T(8,128)(2,1)S(1)}, bf16[1024,128]{1,0:T(8,128)(2,1)}, u32[]{:S(2)}) copy-start(bf16[1024,128]{1,0:T(8,128)(2,1)} %convolution_convert_fusion.1.joint) | copy-start | bytes 786436
  51.7 1.0 copy-start.6
  53.4 6.7 %collective-permute-start.2 = (bf16[128,128]{1,0:T(8,128)(2,1)}, bf16[128,128]{1,0:T(8,128)(2,1)}, u32[]{:S(2)}, u32[]{:S(2)}) collective-permute-start(bf16[128,128]{1,0:T(8,128)(2,1)} %get-tuple-element.38), channel_id=1, source_target_pairs={{0,4},{4,8},{8,12},{1,5},{5,9},{9,13},{2,6},{6,10},{10,14},{3,7},{... | collective-permute-start | bytes 98312 | tf_op jit(solution)/shard_map/ppermute | solution.py:28
  56.7 6.1 %collective-permute-start.3 = (bf16[128,128]{1,0:T(8,128)(2,1)}, bf16[128,128]{1,0:T(8,128)(2,1)}, u32[]{:S(2)}, u32[]{:S(2)}) collective-permute-start(bf16[128,128]{1,0:T(8,128)(2,1)} %get-tuple-element.39), channel_id=1, source_target_pairs={{4,0},{8,4},{12,8},{5,1},{9,5},{13,9},{6,2},{10,6},{14,10},{7,3},{... | collective-permute-start | bytes 98312 | tf_op jit(solution)/shard_map/ppermute | solution.py:29
  76.3 1.0 copy-start.10
  76.3 1.0 copy-start.12
  77.3 11.3 %copy-start.7 = (bf16[512,1024]{1,0:T(8,128)(2,1)S(1)}, bf16[512,1024]{1,0:T(8,128)(2,1)}, u32[]{:S(2)}) copy-start(bf16[512,1024]{1,0:T(8,128)(2,1)} %copy-done.6) | copy-start | bytes 3145732
  79.5 4.8 %collective-permute-start.4 = (f32[128,128]{1,0:T(8,128)S(1)}, f32[128,128]{1,0:T(8,128)S(1)}, u32[]{:S(2)}, u32[]{:S(2)}) collective-permute-start(f32[128,128]{1,0:T(8,128)S(1)} %get-tuple-element.37), channel_id=1, source_target_pairs={{0,4},{4,8},{8,12},{1,5},{5,9},{9,13},{2,6},{6,10},{10,14},{3,7},{... | collective-permute-start | bytes 196616 | tf_op jit(solution)/shard_map/ppermute | solution.py:28
  82.4 6.2 %collective-permute-start.5 = (f32[128,128]{1,0:T(8,128)S(1)}, f32[128,128]{1,0:T(8,128)S(1)}, u32[]{:S(2)}, u32[]{:S(2)}) collective-permute-start(f32[128,128]{1,0:T(8,128)S(1)} %get-tuple-element.36), channel_id=1, source_target_pairs={{4,0},{8,4},{12,8},{5,1},{9,5},{13,9},{6,2},{10,6},{14,10},{7,3},{... | collective-permute-start | bytes 196616 | tf_op jit(solution)/shard_map/ppermute | solution.py:29
  88.6 0.8 copy-start.8
  89.8 1.1 copy-start.5
  89.8 1.1 copy-start.9
Sparse Core Ops, SparseCore 0:
  91.0 91.2 all-reduce.1

commit v2 on v1

--- a/solution.py
+++ b/solution.py
@@ -187,70 +187,374 @@
     return diff * lax.rsqrt(diff * diff + smooth * smooth)
 
 
+def copy_to(source, target, send, arrive, seq, member):
+    return pltpu.make_async_remote_copy(
+        src_ref=source,
+        dst_ref=target,
+        send_sem=send,
+        recv_sem=arrive,
+        device_id={"seq": seq, "member": member},
+        device_id_type=pl.DeviceIdType.MESH,
+    )
+
+
+def tail_kernel(
+    seqs, members, mapped, neighbours, area, tokens_far, attended_far, observed_far, output_far,
+    middle_out, rows_out, decoder_out,
+    every, counts, turned, middle, edges, edges_in, terms, terms_in, sums, sums_in, mine,
+    gathered_rows, gathered, tokens, attended, observed, output_weight,
+    local_sem, field_send, field_in, side_send, side_in, edge_send, edge_in, term_send, term_in,
+    sum_send, sum_in, row_send, row_in, all_send, all_in,
+):
+    s, m = lax.axis_index("seq"), lax.axis_index("member")
+    peers = seqs * members
+    me = s * members + m
+    tok_rows, fields = mapped.shape
+    grid_rows, fan = neighbours.shape
+    wide = tok_rows + 2 * REACH
+    width = tokens.shape[1]
+    chunk = width // peers
+    own = pl.ds(REACH, tok_rows)
+
+    def peer(step):
+        flat = lax.rem(me + step, peers)
+        return flat // members, lax.rem(flat, members)
+
+    barrier = pltpu.get_barrier_semaphore()
+
+    @pl.loop(1, peers)
+    def _(step):
+        seq, member = peer(step)
+        pl.semaphore_signal(
+            barrier, inc=1, device_id={"seq": seq, "member": member},
+            device_id_type=pl.DeviceIdType.MESH,
+        )
+
+    loads = [
+        pltpu.make_async_copy(far, near, local_sem.at[i])
+        for i, (far, near) in enumerate(
+            (
+                (observed_far, observed),
+                (attended_far, attended),
+                (tokens_far, tokens),
+                (output_far, output_weight),
+            )
+        )
+    ]
+    for load in loads:
+        load.start()
+    every[own, 0:fields] = mapped[...].astype(bf16)
+    pl.semaphore_wait(barrier, peers - 1)
+
+    def field_copy(step):
+        lanes = pl.ds(step * fields, fields)
+        return copy_to(
+            every.at[own, pl.ds(0, fields)], every.at[own, lanes],
+            field_send.at[step], field_in.at[step], s, lax.rem(m + step, members),
+        )
+
+    def side_copy(side, step):
+        lanes = pl.ds(step * fields, fields)
+        start, land, seq = ((tok_rows, 0, s + 1), (REACH, REACH + tok_rows, s - 1))[side]
+        return copy_to(
+            every.at[pl.ds(start, REACH), pl.ds(0, fields)],
+            every.at[pl.ds(land, REACH), lanes],
+            side_send.at[side, step], side_in.at[side, step], seq, lax.rem(m + step, members),
+        )
+
+    has_left, has_right = s > 0, s < seqs - 1
+    for step in range(1, members):
+        field_copy(step).start()
+
+    @pl.when(has_right)
+    def _():
+        for step in range(members):
+            side_copy(0, step).start()
+
+    @pl.when(has_left)
+    def _():
+        for step in range(members):
+            side_copy(1, step).start()
+
+    @pl.when(jnp.logical_not(has_left))
+    def _():
+        every[:REACH, :] = jnp.zeros((REACH, members * fields), bf16)
+        edges_in[0] = jnp.zeros((fields, REACH), bf16)
+
+    @pl.when(jnp.logical_not(has_right))
+    def _():
+        every[wide - REACH :, :] = jnp.zeros((REACH, members * fields), bf16)
+        edges_in[1] = jnp.zeros((fields, REACH), bf16)
+
+    base = s * tok_rows - REACH
+    block = 128
+
+    @pl.loop(0, grid_rows // block)
+    def _(i):
+        rows = pl.ds(pl.multiple_of(i * block, block), block)
+        local = neighbours[rows, :] - base
+        place = lax.broadcasted_iota(jnp.int32, (block, wide), 1)
+        total = jnp.zeros((block, wide), f32)
+        for k in range(fan):
+            total += jnp.where(local[:, k : k + 1] == place, 1.0 / fan, 0.0)
+        counts[rows, :] = total.astype(bf16)
+
+    loads[0].wait()
+    for step in range(1, members):
+        field_copy(step).wait()
+
+    @pl.when(has_left)
+    def _():
+        for step in range(members):
+            side_copy(1, step).wait_send()
+            side_copy(0, step).wait_recv()
+
+    @pl.when(has_right)
+    def _():
+        for step in range(members):
+            side_copy(0, step).wait_send()
+            side_copy(1, step).wait_recv()
+
+    @pl.loop(0, grid_rows // block)
+    def _(i):
+        rows = pl.ds(pl.multiple_of(i * block, block), block)
+        found = jnp.dot(counts[rows, :], every[...], preferred_element_type=f32)
+        mean = found[:, :fields]
+        pairs = jnp.zeros((block, fields), f32)
+        for step in range(members):
+            pairs += slope(mean - found[:, step * fields : (step + 1) * fields])
+        single = slope(mean - observed[rows, :])
+        result = area[rows, :] * (
+            single * (1.0 / members) - pairs * (1.0 / (members * (members - 1)))
+        )
+        turned[:, rows] = result.T.astype(bf16)
+
+    def spread(start, size):
+        return jnp.dot(
+            turned[...], counts[:, start : start + size], preferred_element_type=f32
+        )
+
+    edges[0] = spread(0, REACH).astype(bf16)
+    edges[1] = spread(REACH + tok_rows, REACH).astype(bf16)
+
+    def edge_copy(side):
+        return copy_to(
+            edges.at[side], edges_in.at[1 - side], edge_send.at[side], edge_in.at[side],
+            s - 1 if side == 0 else s + 1, m,
+        )
+
+    @pl.when(has_left)
+    def _():
+        edge_copy(0).start()
+
+    @pl.when(has_right)
+    def _():
+        edge_copy(1).start()
+
+    middle[...] = spread(REACH, tok_rows)
+    loads[1].wait()
+    loads[2].wait()
+    inner = middle[:, REACH : tok_rows - REACH].astype(bf16)
+    output_term = jnp.dot(
+        inner, attended[REACH : tok_rows - REACH, :], preferred_element_type=f32
+    )
+
+    @pl.when(has_left)
+    def _():
+        edge_copy(0).wait_send()
+        edge_copy(1).wait_recv()
+
+    @pl.when(has_right)
+    def _():
+        edge_copy(1).wait_send()
+        edge_copy(0).wait_recv()
+
+    middle[:, :REACH] += edges_in[0].astype(f32)
+    middle[:, tok_rows - REACH :] += edges_in[1].astype(f32)
+    whole = middle[...].astype(bf16)
+    output_term += jnp.dot(whole[:, :REACH], attended[:REACH, :], preferred_element_type=f32)
+    output_term += jnp.dot(
+        whole[:, tok_rows - REACH :], attended[tok_rows - REACH :, :],
+        preferred_element_type=f32,
+    )
+
+    def put(part, value):
+        rows = value.T.astype(bf16)
+        for member in range(members):
+            for seq in range(seqs):
+                at = (seq * members + member) * chunk
+                terms[part, member, seq] = rows[at : at + chunk, :]
+
+    def term_copy(part, step):
+        member = lax.rem(m + step, members)
+        return copy_to(
+            terms.at[part, member], terms_in.at[part, step],
+            term_send.at[part, step], term_in.at[part, step], s, member,
+        )
+
+    def sum_copy(part, step):
+        seq = lax.rem(s + step, seqs)
+        return copy_to(
+            sums.at[part, seq], sums_in.at[part, step],
+            sum_send.at[part, step], sum_in.at[part, step], seq, m,
+        )
+
+    put(0, output_term)
+    for step in range(1, members):
+        term_copy(0, step).start()
+    decoder_term = jnp.dot(whole, tokens[...], preferred_element_type=f32)
+    loads[3].wait()
+    decoder_term += jnp.dot(
+        output_term.astype(bf16), output_weight[...], preferred_element_type=f32
+    )
+    put(1, decoder_term)
+    for step in range(1, members):
+        term_copy(1, step).start()
+    middle_out[...] = middle[...].T.astype(bf16)
+    for part in range(2):
+        for step in range(1, members):
+            term_copy(part, step).wait()
+        total = terms[part, m].astype(f32)
+        for step in range(1, members):
+            total += terms_in[part, step].astype(f32)
+        sums[part] = total.astype(bf16)
+
+        @pl.loop(1, seqs)
+        def _(step):
+            sum_copy(part, step).start()
+
+    def row_copy(step):
+        return copy_to(
+            mine.at[0], gathered_rows.at[m], row_send.at[step], row_in.at[step],
+            s, lax.rem(m + step, members),
+        )
+
+    def all_copy(step):
+        seq, member = peer(step)
+        return copy_to(
+            mine.at[1], gathered.at[me], all_send.at[step], all_in.at[step], seq, member
+        )
+
+    for part in range(2):
+
+        @pl.loop(1, seqs)
+        def _(step):
+            sum_copy(part, step).wait()
+
+        total = sums[part, s].astype(f32)
+        for step in range(1, seqs):
+            total += sums_in[part, step].astype(f32)
+        mine[part] = total.astype(bf16)
+        if part == 0:
+            for step in range(1, members):
+                row_copy(step).start()
+        else:
+
+            @pl.loop(1, peers)
+            def _(step):
+                all_copy(step).start()
+
+    gathered_rows[m] = mine[0]
+    gathered[me] = mine[1]
+    for step in range(1, members):
+        row_copy(step).wait()
+    rows_out[...] = gathered_rows[...]
+
+    @pl.loop(1, peers)
+    def _(step):
+        all_copy(step).wait()
+
+    decoder_out[...] = gathered[...]
+
+
+def finish(mapped, neighbours, area, tokens, attended, observed, output_weight, seqs, members):
+    tok_rows, width = tokens.shape
+    fields = mapped.shape[1]
+    grid_rows = neighbours.shape[0]
+    wide = tok_rows + 2 * REACH
+    peers = seqs * members
+    chunk = width // peers
+    near = pl.BlockSpec(memory_space=pltpu.VMEM)
+    far = pl.BlockSpec(memory_space=pl.ANY)
+    dma = pltpu.SemaphoreType.DMA
+    return pl.pallas_call(
+        functools.partial(tail_kernel, seqs, members),
+        in_specs=[near] * 3 + [far] * 4,
+        out_specs=[near] * 3,
+        out_shape=[
+            jax.ShapeDtypeStruct((tok_rows, fields), bf16),
+            jax.ShapeDtypeStruct((members, chunk, fields), bf16),
+            jax.ShapeDtypeStruct((peers, chunk, fields), bf16),
+        ],
+        scratch_shapes=[
+            pltpu.VMEM((wide, members * fields), bf16),
+            pltpu.VMEM((grid_rows, wide), bf16),
+            pltpu.VMEM((fields, grid_rows), bf16),
+            pltpu.VMEM((fields, tok_rows), f32),
+            pltpu.VMEM((2, fields, REACH), bf16),
+            pltpu.VMEM((2, fields, REACH), bf16),
+            pltpu.VMEM((2, members, seqs, chunk, fields), bf16),
+            pltpu.VMEM((2, members, seqs, chunk, fields), bf16),
+            pltpu.VMEM((2, seqs, chunk, fields), bf16),
+            pltpu.VMEM((2, seqs, chunk, fields), bf16),
+            pltpu.VMEM((2, chunk, fields), bf16),
+            pltpu.VMEM((members, chunk, fields), bf16),
+            pltpu.VMEM((peers, chunk, fields), bf16),
+            pltpu.VMEM(tokens.shape, bf16),
+            pltpu.VMEM(attended.shape, bf16),
+            pltpu.VMEM(observed.shape, f32),
+            pltpu.VMEM(output_weight.shape, bf16),
+            dma((4,)),
+            dma((members,)),
+            dma((members,)),
+            dma((2, members)),
+            dma((2, members)),
+            dma((2,)),
+            dma((2,)),
+            dma((2, members)),
+            dma((2, members)),
+            dma((2, seqs)),
+            dma((2, seqs)),
+            dma((members,)),
+            dma((members,)),
+            dma((peers,)),
+            dma((peers,)),
+        ],
+        compiler_params=pltpu.CompilerParams(
+            vmem_limit_bytes=48 << 20, collective_id=0, has_side_effects=True
+        ),
+    )(mapped, neighbours, area, tokens, attended, observed, output_weight)
+
+
 def body(tokens, input_weight, output_weight, decoder_weight, neighbours, observed, cell_area):
     own_tokens = tokens[0]
     tok_rows, width = own_tokens.shape
-    fields_count = decoder_weight.shape[1]
-    seq_count = lax.axis_size("seq")
+    fields = decoder_weight.shape[1]
+    seqs = lax.axis_size("seq")
     members = lax.axis_size("member")
     seq_place = lax.axis_index("seq")
-    fan_count = neighbours.shape[1]
     grid_rows = neighbours.shape[0]
-    wide_rows = tok_rows + 2 * REACH
 
     before, after = from_sides(own_tokens, WINDOW // 2)
     own = project([own_tokens], input_weight, 0)
     joint = jnp.dot(output_weight, decoder_weight, preferred_element_type=f32).astype(bf16)
-    local = neighbours - (seq_place * tok_rows - REACH)
-    places = jnp.arange(wide_rows, dtype=jnp.int32)
-    counts = jnp.zeros((grid_rows, wide_rows), f32)
-    for column in range(fan_count):
-        counts = counts + (local[:, column][:, None] == places[None, :]).astype(f32)
-    counts = (counts / fan_count).astype(bf16)
     side = project([before, after], input_weight, width // COLS)
-    ends = jnp.stack([seq_place > 0, seq_place < seq_count - 1]).astype(jnp.int32)
+    ends = jnp.stack([seq_place > 0, seq_place < seqs - 1]).astype(jnp.int32)
     attended, mapped = attend(ends, own, side, own_tokens, decoder_weight, joint)
-
-    mapped = mapped.astype(bf16)
-    before, after = from_sides(mapped, REACH)
-    mapped = jnp.concatenate([before, mapped, after], axis=0)
-    every = lax.all_gather(mapped, "member", axis=0, tiled=False)
-    all_fields = jnp.einsum("gt,mtf->mgf", counts, every, preferred_element_type=f32)
-    fields = lax.dynamic_index_in_dim(all_fields, lax.axis_index("member"), 0, keepdims=False)
-    pairs = jnp.sum(slope(fields[None] - all_fields), axis=0)
-    single = slope(fields - observed)
-    cotangent = (
-        cell_area[:, None] * (single / members - pairs / (members * (members - 1)))
-    ).astype(bf16)
-    spread = lax.dot_general(
-        counts, cotangent, (((0,), (0,)), ((), ())), preferred_element_type=f32
-    )
-    edges = jnp.concatenate([spread[:REACH], spread[REACH + tok_rows :]], axis=0)
-    before, after = from_sides(edges, REACH)
-    middle = spread[REACH : REACH + tok_rows]
-    middle = middle.at[:REACH].add(before).at[tok_rows - REACH :].add(after).astype(bf16)
+    middle, rows, decoder_sum = finish(
+        mapped, neighbours, cell_area[:, None], own_tokens, attended, observed, output_weight,
+        seqs, members,
+    )
     attention_cotangent = lax.dot_general(
         middle, joint, (((1,), (1,)), ((), ())), preferred_element_type=f32
     ).astype(bf16)
-    output_term = lax.dot_general(
-        attended, middle, (((0,), (0,)), ((), ())), preferred_element_type=f32
-    )
-    decoder_term = lax.dot_general(
-        own_tokens, middle, (((0,), (0,)), ((), ())), preferred_element_type=f32
-    ) + lax.dot_general(
-        output_weight, output_term.astype(bf16), (((0,), (0,)), ((), ())),
+    output_gradient = lax.dot_general(
+        rows.reshape(width // seqs, fields), decoder_weight, (((1,), (1,)), ((), ())),
         preferred_element_type=f32,
-    )
-    both = lax.psum(
-        jnp.concatenate([output_term, decoder_term], axis=1), ("seq", "member")
-    )
-    decoder_gradient = both[:, fields_count:] / math.sqrt(members * grid_rows * seq_count)
-    rows = width // seq_count
-    output_rows = lax.dynamic_slice_in_dim(both[:, :fields_count], seq_place * rows, rows, 0)
-    output_gradient = lax.dot_general(
-        output_rows.astype(bf16), decoder_weight, (((1,), (1,)), ((), ())),
-        preferred_element_type=f32,
-    ) / math.sqrt(members * tok_rows * seq_count)
+    ) * (1.0 / math.sqrt(members * tok_rows * seqs))
+    decoder_gradient = decoder_sum.reshape(width, fields).astype(f32) * (
+        1.0 / math.sqrt(members * grid_rows * seqs)
+    )
     return (attention_cotangent[None], output_gradient, decoder_gradient)
 
 

time: 194 us -> 84 us (0.43)
  waiting for transfers between devices: 99.6 us -> 1.48 us
  Pallas kernels: 27.8 us -> 63.4 us
  between operations: 14.4 us -> 0.79 us
  starting transfers between devices: 15.8 us -> 6.37 us
  blocking collectives: 8.58 us -> 0 us
  matrix products: 12.5 us -> 4.97 us
  local copies, waits for them, and re-layouts: 11.6 us -> 5.52 us
  other arithmetic: 3.44 us -> 0.93 us
    psum x1 -> x0, waiting for transfers between devices: 90 us -> none  [body(): lax.psum(jnp.concatenate([output_term, decoder_term], axis=1), ('seq', 'm...]
    pallas_call x0 -> x1, Pallas kernels: none -> 36.7 us  [finish(): pl.pallas_call(functools.partial(tail_kernel, seqs, members), in_specs=[n...]
    all_gather x1 -> x0, blocking collectives: 8.58 us -> none  [body(): every = lax.all_gather(mapped, 'member', axis=0, tiled=False)]
    ppermute x3 -> x1, waiting for transfers between devices: 9.02 us -> 1.48 us  [from_sides(): lax.ppermute(cells[:width], 'seq', left)]
    dot_general x6 -> x1, matrix products: 8.69 us -> 1.27 us  [body(): lax.dot_general(rows.reshape(width // seqs, fields), decoder_weight, (((1...]
    ppermute x3 -> x1, starting transfers between devices: 11.9 us -> 5.08 us  [from_sides(): lax.ppermute(cells[rows - width:], 'seq', right)]
    unnamed x28 -> x13, local copies, waits for them, and re-layouts: 7.43 us -> 3.02 us
    ppermute x3 -> x1, starting transfers between devices: 3.85 us -> 1.29 us  [from_sides(): lax.ppermute(cells[:width], 'seq', left)]
  transfers between devices with their start and end apart: 7 -> 2, of which waited for: 5 -> 1; matrix products, arithmetic and copies ran while one was open for 3% -> 3% of each run, Pallas kernels for 4% -> 8%
where the time goes in v2:
time: 84 us; the launch traced here: 83.4 us
  Pallas kernels  63.4 us (75%)
  starting transfers between devices  6.37 us (8%)
  local copies, waits for them, and re-layouts  5.52 us (7%)
  matrix products  4.97 us (6%)
  waiting for transfers between devices  1.48 us (2%)
  other arithmetic  0.93 us (1%)
    pallas_call x1, Pallas kernels, finish(): pl.pallas_call(functools.partial(tail_kernel, seqs, members), in_specs=[n...  36.7 us
    pallas_call x1, Pallas kernels, attend(): pl.pallas_call(attend_kernel, grid=(steps,), in_specs=[pl.BlockSpec(memor...  14.9 us
    pallas_call x2, Pallas kernels, project(): pl.pallas_call(functools.partial(project_kernel, first, width), grid=(ste...  11.7 us
    ppermute x1, starting transfers between devices, from_sides(): lax.ppermute(cells[rows - width:], 'seq', right)  5.08 us
    unnamed x13, local copies, waits for them, and re-layouts  3.02 us
    dot_general x1, matrix products, body(): jnp.dot(output_weight, decoder_weight, preferred_element_type=f32)  2.29 us
    slice x1, local copies, waits for them, and re-layouts, from_sides(): cells[:width]  2.28 us
  transfers between devices with their start and end apart: 2, of which 1 were waited for; matrix products, arithmetic and copies ran while one was open for 3% of the time, Pallas kernels for 8%

profile of v2, /device:TPU:0, one launch (start us, length us, event | category | flops | bytes accessed | tf_op | source)
XLA Modules:
  0.0 83.4 jit_solution(16184899676186076465)
XLA Ops:
  0.6 0.0 copy-start.4
  0.6 0.0 copy-start.5
  0.7 0.0 copy-start.2
  0.7 2.3 %slice_bitcast_fusion = (bf16[256,1024]{1,0:T(8,128)(2,1)}, bf16[256,1024]{1,0:T(8,128)(2,1)}) fusion(bf16[1,512,1024]{2,1,0:T(8,128)(2,1)} %param.7), kind=kLoop, calls=%fused_computation.5 | loop fusion | bytes 2097152 | tf_op jit(solution)/shard_map/slice | solution.py:29
  2.9 0.0 copy-start
  2.9 5.1 %collective-permute-start = (bf16[256,1024]{1,0:T(8,128)(2,1)}, bf16[256,1024]{1,0:T(8,128)(2,1)S(1)}, u32[]{:S(2)}, u32[]{:S(2)}) collective-permute-start(bf16[256,1024]{1,0:T(8,128)(2,1)} %get-tuple-element.14), channel_id=1, source_target_pairs={{0,4},{4,8},{8,12},{1,5},{5,9},{9,13},{2,6},{6,10},{10,14},{3,7},{... | collective-permute-start | bytes 1572872 | tf_op jit(solution)/shard_map/ppermute | solution.py:28
  8.0 1.3 %collective-permute-start.1 = (bf16[256,1024]{1,0:T(8,128)(2,1)}, bf16[256,1024]{1,0:T(8,128)(2,1)S(1)}, u32[]{:S(2)}, u32[]{:S(2)}) collective-permute-start(bf16[256,1024]{1,0:T(8,128)(2,1)} %get-tuple-element.13), channel_id=1, source_target_pairs={{4,0},{8,4},{12,8},{5,1},{9,5},{13,9},{6,2},{10,6},{14,10},{7,3},{... | collective-permute-start | bytes 1572872 | tf_op jit(solution)/shard_map/ppermute | solution.py:29
  9.3 0.0 copy-done.4
  9.3 0.2 copy.11.neighbours
  9.6 0.0 copy-done.5
  9.6 0.2 copy.12.area
  9.8 0.1 add_convert_fusion.ends
  9.9 0.0 copy-done.2
  9.9 2.3 %convolution_convert_fusion.1.joint = bf16[1024,128]{1,0:T(8,128)(2,1)S(1)} fusion(bf16[1024,1024]{1,0:T(8,128)(2,1)} %output_far.1, bf16[1024,128]{1,0:T(8,128)(2,1)S(1)} %copy-done.2), kind=kOutput, calls=%fused_computation.3 | convolution fusion | flops 268566528 | bytes 2621440 | tf_op jit(solution)/shard_map/dot_general | solution.py:540
  12.2 0.0 copy-done
  12.2 0.0 copy-start.1
  12.2 2.8 %copy-done.1 = bf16[1024,3072]{1,0:T(8,128)(2,1)S(1)} copy-done((bf16[1024,3072]{1,0:T(8,128)(2,1)S(1)}, bf16[1024,3072]{1,0:T(8,128)(2,1)}, u32[]{:S(2)}) %copy-start.1) | copy-done | bytes 6291480
  15.0 7.0 %shard_map.94.query.key_own.value_own = bf16[512,3072]{1,0:T(8,128)(2,1)S(1)} custom-call(bf16[512,1024]{1,0:T(8,128)(2,1)S(1)} %bitcast.18, bf16[1024,3072]{1,0:T(8,128)(2,1)S(1)} %copy-done.1), custom_call_target="tpu_custom_call" | custom-call | flops 3221225472 | bytes 10485760 | tf_op jit(solution)/shard_map/pallas_call | solution.py:76
  22.0 0.0 collective-permute-done.refs_0_
  22.0 1.5 %collective-permute-done.1.refs_1_ = bf16[256,1024]{1,0:T(8,128)(2,1)S(1)} collective-permute-done((bf16[256,1024]{1,0:T(8,128)(2,1)}, bf16[256,1024]{1,0:T(8,128)(2,1)S(1)}, u32[]{:S(2)}, u32[]{:S(2)}) %collective-permute-start.1) | collective-permute-done | bytes 524320 | tf_op jit(solution)/shard_map/ppermute | solution.py:29
  23.5 4.7 %shard_map.95.key_side.value_side = bf16[512,2048]{1,0:T(8,128)(2,1)S(1)} custom-call(bf16[256,1024]{1,0:T(8,128)(2,1)S(1)} %collective-permute-done.refs_0_, bf16[256,1024]{1,0:T(8,128)(2,1)S(1)} %collective-permute-done.1.refs_1_, bf16[1024,3072]{1,0:T(8,128)(2,1)S(1)} %copy-done.1), custom_call_target="tpu_custom_call" | custom-call | flops 2147483648 | bytes 7340032 | tf_op jit(solution)/shard_map/pallas_call | solution.py:76
  28.2 0.0 copy-start.3
  28.3 14.9 %shard_map.96 = (bf16[512,1024]{1,0:T(8,128)(2,1)S(1)}, f32[512,128]{1,0:T(8,128)S(1)}) custom-call(s32[2]{0:T(128)S(1)} %add_convert_fusion.ends, bf16[512,3072]{1,0:T(8,128)(2,1)S(1)} %shard_map.94.query.key_own.value_own, bf16[512,3072]{1,0:T(8,128)(2,1)S(1)} %shard_map.94.query.key_own.value_own, bf16[512,2048]{1,0:T(8,128)(2,1)S(1)} %shard_map.95.key_side.value_side, ...), custom_call_target="tpu_custom_call" | custom-call | tf_op jit(solution)/shard_map/pallas_call | solution.py:159
  43.2 0.0 copy-done.3
  43.2 36.7 %shard_map.97 = (bf16[512,128]{1,0:T(8,128)(2,1)S(1)}, bf16[4,64,128]{2,1,0:T(8,128)(2,1)S(1)}, bf16[16,64,128]{2,1,0:T(8,128)(2,1)S(1)}) custom-call(f32[512,128]{1,0:T(8,128)S(1)} %get-tuple-element.8.mapped, s32[1024,4]{1,0:T(8,128)S(1)} %copy.11.neighbours, f32[1024,1]{1,0:T(8,128)S(1)} %copy.12.area, bf16[512,1024]{1,0:T(8,128)(2,1)S(1)} %bitcast.20, ...), custom_call_target="tpu_custom_call" | custom-call | tf_op jit(solution)/shard_map/pallas_call | solution.py:480
  79.9 1.4 %fusion = bf16[1,512,1024]{2,1,0:T(8,128)(2,1)} fusion(bf16[512,128]{1,0:T(8,128)(2,1)S(1)} %get-tuple-element.10, bf16[1024,128]{1,0:T(8,128)(2,1)S(1)} %convolution_convert_fusion.1.joint), kind=kOutput, calls=%fused_computation.1 | convolution fusion | flops 134742016 | bytes 1441792 | tf_op jit(solution)/shard_map/dot_general | solution.py:548
  81.3 1.3 %convolution_multiply_fusion = f32[256,1024]{1,0:T(8,128)} fusion(bf16[256,128]{1,0:T(8,128)(2,1)S(1)} %bitcast.21, bf16[1024,128]{1,0:T(8,128)(2,1)S(1)} %copy-done.2), kind=kOutput, calls=%fused_computation.2 | convolution fusion | flops 67371008 | bytes 1376256 | tf_op jit(solution)/shard_map/dot_general | solution.py:551
  82.6 0.8 %convert_multiply_fusion = f32[16,64,128]{2,1,0:T(8,128)} fusion(bf16[16,64,128]{2,1,0:T(8,128)(2,1)S(1)} %get-tuple-element.12), kind=kLoop, calls=%fused_computation.4 | loop fusion | flops 262144 | bytes 786432 | tf_op jit(solution)/shard_map/mul | solution.py:555
Async XLA Ops:
  0.6 8.7 %copy-start.4 = (s32[1024,4]{0,1:T(4,128)S(1)}, s32[1024,4]{0,1:T(4,128)}, u32[]{:S(2)}) copy-start(s32[1024,4]{0,1:T(4,128)} %param.11) | copy-start | bytes 49156
  0.6 8.9 %copy-start.5 = (f32[1024]{0:T(1024)S(1)}, f32[1024]{0:T(1024)}, u32[]{:S(2)}) copy-start(f32[1024]{0:T(1024)} %param.13) | copy-start | bytes 12292
  0.7 9.2 %copy-start.2 = (bf16[1024,128]{1,0:T(8,128)(2,1)S(1)}, bf16[1024,128]{1,0:T(8,128)(2,1)}, u32[]{:S(2)}) copy-start(bf16[1024,128]{1,0:T(8,128)(2,1)} %decoder.1) | copy-start | bytes 786436
  2.9 9.3 %copy-start = (bf16[1,512,1024]{2,1,0:T(8,128)(2,1)S(1)}, bf16[1,512,1024]{2,1,0:T(8,128)(2,1)}, u32[]{:S(2)}) copy-start(bf16[1,512,1024]{2,1,0:T(8,128)(2,1)} %param.7) | copy-start | bytes 3145732
  2.9 19.1 %collective-permute-start = (bf16[256,1024]{1,0:T(8,128)(2,1)}, bf16[256,1024]{1,0:T(8,128)(2,1)S(1)}, u32[]{:S(2)}, u32[]{:S(2)}) collective-permute-start(bf16[256,1024]{1,0:T(8,128)(2,1)} %get-tuple-element.14), channel_id=1, source_target_pairs={{0,4},{4,8},{8,12},{1,5},{5,9},{9,13},{2,6},{6,10},{10,14},{3,7},{... | collective-permute-start | bytes 1572872 | tf_op jit(solution)/shard_map/ppermute | solution.py:28
  8.0 15.5 %collective-permute-start.1 = (bf16[256,1024]{1,0:T(8,128)(2,1)}, bf16[256,1024]{1,0:T(8,128)(2,1)S(1)}, u32[]{:S(2)}, u32[]{:S(2)}) collective-permute-start(bf16[256,1024]{1,0:T(8,128)(2,1)} %get-tuple-element.13), channel_id=1, source_target_pairs={{4,0},{8,4},{12,8},{5,1},{9,5},{13,9},{6,2},{10,6},{14,10},{7,3},{... | collective-permute-start | bytes 1572872 | tf_op jit(solution)/shard_map/ppermute | solution.py:29
  12.2 2.8 %copy-start.1 = (bf16[1024,3072]{1,0:T(8,128)(2,1)S(1)}, bf16[1024,3072]{1,0:T(8,128)(2,1)}, u32[]{:S(2)}) copy-start(bf16[1024,3072]{1,0:T(8,128)(2,1)} %refs_2_.1) | copy-start | bytes 18874372
  28.2 14.9 %copy-start.3 = (f32[1024,128]{1,0:T(8,128)S(1)}, f32[1024,128]{1,0:T(8,128)}, u32[]{:S(2)}) copy-start(f32[1024,128]{1,0:T(8,128)} %observed_far.1) | copy-start | bytes 1572868

commit v3 on v2

v3 whole, which is shorter than its diff:
```python
import functools
import math

import jax
import jax.numpy as jnp
from jax import lax
from jax.experimental import pallas as pl
from jax.experimental.pallas import tpu as pltpu
from jax.sharding import PartitionSpec as P

HEAD_DIM = 64
WINDOW = 512
REACH = 128
LANES = 128
COLS = 512

smooth = 0.1
f32 = jnp.float32
bf16 = jnp.bfloat16


def normalize(rows):
    values = rows.astype(f32)
    centre = jnp.mean(values, axis=-1, keepdims=True)
    values = values - centre
    spread = jnp.mean(values * values, axis=-1, keepdims=True)
    return (values * lax.rsqrt(spread + 1e-05)).astype(bf16)


def place_columns(mixed, scale):
    side = 256
    down = lax.broadcasted_iota(jnp.int32, (side, side), 0) >> 6
    across = lax.broadcasted_iota(jnp.int32, (side, side), 1) >> 6
    same = jnp.where(down == across, 1.0 / HEAD_DIM, 0.0).astype(bf16)
    pieces = []
    for at in range(0, mixed.shape[1], side):
        piece = mixed[:, at : at + side]
        mean = jnp.dot((piece * piece).astype(bf16), same, preferred_element_type=f32)
        pieces.append((piece * (lax.rsqrt(mean + 1e-06) * scale)).astype(bf16))
    return jnp.concatenate(pieces, axis=1)


def project(normed, weight, out, first, waits):
    width = weight.shape[0]
    for at in range(first, weight.shape[1], COLS):
        if waits:
            waits[at // COLS].wait()
        mixed = jnp.dot(normed[...], weight[:, at : at + COLS], preferred_element_type=f32)
        if at < 2 * width:
            mixed = place_columns(mixed, HEAD_DIM**-0.5 if at < width else 1.0)
        out[:, at - first : at - first + COLS] = mixed.astype(bf16)


def attend(own, side, joint, attended, mapped, keys, values, has_left, has_right):
    half = WINDOW // 2
    rows, width = attended.shape
    first = lax.broadcasted_iota(jnp.int32, (1, LANES), 1) < HEAD_DIM
    block = half
    part_rows = block // 2
    span = block + WINDOW
    part_span = part_rows + WINDOW
    down = lax.broadcasted_iota(jnp.int32, (part_rows, part_rows), 0)
    across = lax.broadcasted_iota(jnp.int32, (part_rows, part_rows), 1)
    late = across >= down
    exists = (
        jnp.where(has_left, 1.0, 0.0).astype(f32), 1.0, jnp.where(has_right, 1.0, 0.0).astype(f32)
    )

    @pl.loop(0, width // LANES)
    def _(j):
        def at(offset):
            return pl.ds(pl.multiple_of(j * LANES + offset, LANES), LANES)

        keys[:half, :] = side[:half, at(0)]
        keys[half : half + rows, :] = own[:, at(width)]
        keys[half + rows :, :] = side[half:, at(0)]
        chunks = (
            (0, side[:half, at(width)]),
            (half, own[:, at(2 * width)]),
            (half + rows, side[half:, at(width)]),
        )
        for (begin, part), there in zip(chunks, exists):
            ones = jnp.full(part.shape, there, f32).astype(bf16)
            values[0, begin : begin + part.shape[0], :] = jnp.where(first, part, ones)
            values[1, begin : begin + part.shape[0], :] = jnp.where(first, ones, part)
        for start in range(0, rows, block):
            query = own[start : start + block, at(0)]
            here = keys[start : start + span, :]
            sums = []
            for head in range(2):
                part = jnp.where(first == (head == 0), query, jnp.zeros_like(query))
                scores = lax.dot_general(
                    part, here, (((1,), (1,)), ((), ())), preferred_element_type=f32
                )
                lines = []
                for line in range(2):
                    begin = line * part_rows
                    weights = jnp.exp(
                        scores[begin : begin + part_rows, begin : begin + part_span]
                    )
                    blank = jnp.zeros((part_rows, part_rows), bf16)
                    pieces = [
                        jnp.where(late, weights[:, :part_rows], 0.0).astype(bf16),
                        weights[:, part_rows : part_span - part_rows].astype(bf16),
                        jnp.where(late, 0.0, weights[:, part_span - part_rows :]).astype(bf16),
                    ]
                    pieces = pieces + [blank] if line == 0 else [blank] + pieces
                    lines.append(jnp.concatenate(pieces, axis=1))
                total = jnp.dot(
                    jnp.concatenate(lines, axis=0),
                    values[head, start : start + span, :],
                    preferred_element_type=f32,
                )
                sums.append(total / pltpu.roll(total, HEAD_DIM, 1))
            result = jnp.where(first, sums[0], sums[1]).astype(bf16)
            attended[start : start + block, at(0)] = result
            mapped[start : start + block, :] += jnp.dot(
                result, joint[at(0), :], preferred_element_type=f32
            )


def slope(diff):
    return diff * lax.rsqrt(diff * diff + smooth * smooth)


def copy_to(source, target, send, arrive, seq, member):
    return pltpu.make_async_remote_copy(
        src_ref=source,
        dst_ref=target,
        send_sem=send,
        recv_sem=arrive,
        device_id={"seq": seq, "member": member},
        device_id_type=pl.DeviceIdType.MESH,
    )


def layer_kernel(
    seqs, members, decoder, neighbours, area, tokens_far, weight_far, observed_far, output_far,
    middle_out, rows_out, decoder_out, joint,
    every, counts, turned, middle, edges, edges_in, terms, terms_in, sums, sums_in, mine,
    gathered_rows, gathered, tokens, attended, observed, output_weight,
    weight, normed, beside, own_parts, side_parts, mapped, keys, values, halo_send, halo_in,
    local_sem, field_send, field_in, side_send, side_in, edge_send, edge_in, term_send, term_in,
    sum_send, sum_in, row_send, row_in, all_send, all_in,
):
    s, m = lax.axis_index("seq"), lax.axis_index("member")
    peers = seqs * members
    me = s * members + m
    tok_rows, fields = mapped.shape
    grid_rows, fan = neighbours.shape
    wide = tok_rows + 2 * REACH
    width = tokens.shape[1]
    chunk = width // peers
    own = pl.ds(REACH, tok_rows)

    def peer(step):
        flat = lax.rem(me + step, peers)
        return flat // members, lax.rem(flat, members)

    barrier = pltpu.get_barrier_semaphore()

    @pl.loop(1, peers)
    def _(step):
        seq, member = peer(step)
        pl.semaphore_signal(
            barrier, inc=1, device_id={"seq": seq, "member": member},
            device_id_type=pl.DeviceIdType.MESH,
        )

    columns = weight.shape[1] // COLS
    loads = [
        pltpu.make_async_copy(far, near, local_sem.at[i])
        for i, (far, near) in enumerate(
            [(tokens_far, tokens)]
            + [
                (weight_far.at[:, pl.ds(i * COLS, COLS)], weight.at[:, pl.ds(i * COLS, COLS)])
                for i in range(columns)
            ]
            + [(output_far, output_weight), (observed_far, observed)]
        )
    ]
    for load in loads:
        load.start()
    has_left, has_right = s > 0, s < seqs - 1
    half = WINDOW // 2

    def halo_copy(to_right):
        start, land, seq = (tok_rows - half, 0, s + 1) if to_right else (0, half, s - 1)
        return copy_to(
            tokens_far.at[pl.ds(start, half), :], beside.at[pl.ds(land, half), :],
            halo_send.at[to_right], halo_in.at[to_right], seq, m,
        )

    @pl.when(jnp.logical_not(has_left))
    def _():
        beside[:half, :] = jnp.zeros((half, width), bf16)

    @pl.when(jnp.logical_not(has_right))
    def _():
        beside[half:, :] = jnp.zeros((half, width), bf16)

    pl.semaphore_wait(barrier, peers - 1)

    @pl.when(has_right)
    def _():
        halo_copy(1).start()

    @pl.when(has_left)
    def _():
        halo_copy(0).start()

    loads[0].wait()
    normed[...] = normalize(tokens[...])
    project(normed, weight, own_parts, 0, loads[1 : 1 + columns])
    loads[1 + columns].wait()
    joint[...] = jnp.dot(
        output_weight[...], decoder[...], preferred_element_type=f32
    ).astype(bf16)
    mapped[...] = jnp.dot(tokens[...], decoder[...], preferred_element_type=f32)
    base = s * tok_rows - REACH
    block = 128

    @pl.loop(0, grid_rows // block)
    def _(i):
        rows = pl.ds(pl.multiple_of(i * block, block), block)
        local = neighbours[rows, :] - base
        place = lax.broadcasted_iota(jnp.int32, (block, wide), 1)
        total = jnp.zeros((block, wide), f32)
        for k in range(fan):
            total += jnp.where(local[:, k : k + 1] == place, 1.0 / fan, 0.0)
        counts[rows, :] = total.astype(bf16)

    @pl.when(has_left)
    def _():
        halo_copy(0).wait_send()
        halo_copy(1).wait_recv()

    @pl.when(has_right)
    def _():
        halo_copy(1).wait_send()
        halo_copy(0).wait_recv()

    normed[...] = normalize(beside[...])
    project(normed, weight, side_parts, width, None)
    attend(
        own_parts, side_parts, joint, attended, mapped, keys, values, has_left, has_right
    )
    every[own, 0:fields] = mapped[...].astype(bf16)

    def field_copy(step):
        lanes = pl.ds(step * fields, fields)
        return copy_to(
            every.at[own, pl.ds(0, fields)], every.at[own, lanes],
            field_send.at[step], field_in.at[step], s, lax.rem(m + step, members),
        )

    def side_copy(side, step):
        lanes = pl.ds(step * fields, fields)
        start, land, seq = ((tok_rows, 0, s + 1), (REACH, REACH + tok_rows, s - 1))[side]
        return copy_to(
            every.at[pl.ds(start, REACH), pl.ds(0, fields)],
            every.at[pl.ds(land, REACH), lanes],
            side_send.at[side, step], side_in.at[side, step], seq, lax.rem(m + step, members),
        )

    for step in range(1, members):
        field_copy(step).start()

    @pl.when(has_right)
    def _():
        for step in range(members):
            side_copy(0, step).start()

    @pl.when(has_left)
    def _():
        for step in range(members):
            side_copy(1, step).start()

    @pl.when(jnp.logical_not(has_left))
    def _():
        every[:REACH, :] = jnp.zeros((REACH, members * fields), bf16)
        edges_in[0] = jnp.zeros((fields, REACH), bf16)

    @pl.when(jnp.logical_not(has_right))
    def _():
        every[wide - REACH :, :] = jnp.zeros((REACH, members * fields), bf16)
        edges_in[1] = jnp.zeros((fields, REACH), bf16)

    loads[2 + columns].wait()
    for step in range(1, members):
        field_copy(step).wait()

    @pl.when(has_left)
    def _():
        for step in range(members):
            side_copy(1, step).wait_send()
            side_copy(0, step).wait_recv()

    @pl.when(has_right)
    def _():
        for step in range(members):
            side_copy(0, step).wait_send()
            side_copy(1, step).wait_recv()

    @pl.loop(0, grid_rows // block)
    def _(i):
        rows = pl.ds(pl.multiple_of(i * block, block), block)
        found = jnp.dot(counts[rows, :], every[...], preferred_element_type=f32)
        mean = found[:, :fields]
        pairs = jnp.zeros((block, fields), f32)
        for step in range(members):
            pairs += slope(mean - found[:, step * fields : (step + 1) * fields])
        single = slope(mean - observed[rows, :])
        result = area[rows, :] * (
            single * (1.0 / members) - pairs * (1.0 / (members * (members - 1)))
        )
        turned[:, rows] = result.T.astype(bf16)

    def spread(start, size):
        return jnp.dot(
            turned[...], counts[:, start : start + size], preferred_element_type=f32
        )

    edges[0] = spread(0, REACH).astype(bf16)
    edges[1] = spread(REACH + tok_rows, REACH).astype(bf16)

    def edge_copy(side):
        return copy_to(
            edges.at[side], edges_in.at[1 - side], edge_send.at[side], edge_in.at[side],
            s - 1 if side == 0 else s + 1, m,
        )

    @pl.when(has_left)
    def _():
        edge_copy(0).start()

    @pl.when(has_right)
    def _():
        edge_copy(1).start()

    middle[...] = spread(REACH, tok_rows)
    inner = middle[:, REACH : tok_rows - REACH].astype(bf16)
    output_term = jnp.dot(
        inner, attended[REACH : tok_rows - REACH, :], preferred_element_type=f32
    )

    @pl.when(has_left)
    def _():
        edge_copy(0).wait_send()
        edge_copy(1).wait_recv()

    @pl.when(has_right)
    def _():
        edge_copy(1).wait_send()
        edge_copy(0).wait_recv()

    middle[:, :REACH] += edges_in[0].astype(f32)
    middle[:, tok_rows - REACH :] += edges_in[1].astype(f32)
    whole = middle[...].astype(bf16)
    output_term += jnp.dot(whole[:, :REACH], attended[:REACH, :], preferred_element_type=f32)
    output_term += jnp.dot(
        whole[:, tok_rows - REACH :], attended[tok_rows - REACH :, :],
        preferred_element_type=f32,
    )

    def put(part, value):
        rows = value.T.astype(bf16)
        for member in range(members):
            for seq in range(seqs):
                at = (seq * members + member) * chunk
                terms[part, member, seq] = rows[at : at + chunk, :]

    def term_copy(part, step):
        member = lax.rem(m + step, members)
        return copy_to(
            terms.at[part, member], terms_in.at[part, step],
            term_send.at[part, step], term_in.at[part, step], s, member,
        )

    def sum_copy(part, step):
        seq = lax.rem(s + step, seqs)
        return copy_to(
            sums.at[part, seq], sums_in.at[part, step],
            sum_send.at[part, step], sum_in.at[part, step], seq, m,
        )

    put(0, output_term)
    for step in range(1, members):
        term_copy(0, step).start()
    decoder_term = jnp.dot(whole, tokens[...], preferred_element_type=f32)
    decoder_term += jnp.dot(
        output_term.astype(bf16), output_weight[...], preferred_element_type=f32
    )
    put(1, decoder_term)
    for step in range(1, members):
        term_copy(1, step).start()
    middle_out[...] = middle[...].T.astype(bf16)
    for part in range(2):
        for step in range(1, members):
            term_copy(part, step).wait()
        total = terms[part, m].astype(f32)
        for step in range(1, members):
            total += terms_in[part, step].astype(f32)
        sums[part] = total.astype(bf16)

        @pl.loop(1, seqs)
        def _(step):
            sum_copy(part, step).start()

    def row_copy(step):
        return copy_to(
            mine.at[0], gathered_rows.at[m], row_send.at[step], row_in.at[step],
            s, lax.rem(m + step, members),
        )

    def all_copy(step):
        seq, member = peer(step)
        return copy_to(
            mine.at[1], gathered.at[me], all_send.at[step], all_in.at[step], seq, member
        )

    for part in range(2):

        @pl.loop(1, seqs)
        def _(step):
            sum_copy(part, step).wait()

        total = sums[part, s].astype(f32)
        for step in range(1, seqs):
            total += sums_in[part, step].astype(f32)
        mine[part] = total.astype(bf16)
        if part == 0:
            for step in range(1, members):
                row_copy(step).start()
        else:

            @pl.loop(1, peers)
            def _(step):
                all_copy(step).start()

    gathered_rows[m] = mine[0]
    gathered[me] = mine[1]
    for step in range(1, members):
        row_copy(step).wait()
    rows_out[...] = gathered_rows[...]

    @pl.loop(1, peers)
    def _(step):
        all_copy(step).wait()

    decoder_out[...] = gathered[...]


def layer(decoder, neighbours, area, tokens, weight, observed, output_weight, seqs, members):
    tok_rows, width = tokens.shape
    fields = decoder.shape[1]
    grid_rows = neighbours.shape[0]
    wide = tok_rows + 2 * REACH
    peers = seqs * members
    chunk = width // peers
    near = pl.BlockSpec(memory_space=pltpu.VMEM)
    far = pl.BlockSpec(memory_space=pl.ANY)
    dma = pltpu.SemaphoreType.DMA
    return pl.pallas_call(
        functools.partial(layer_kernel, seqs, members),
        in_specs=[near] * 3 + [far] * 4,
        out_specs=[near] * 4,
        out_shape=[
            jax.ShapeDtypeStruct((tok_rows, fields), bf16),
            jax.ShapeDtypeStruct((members, chunk, fields), bf16),
            jax.ShapeDtypeStruct((peers, chunk, fields), bf16),
            jax.ShapeDtypeStruct((width, fields), bf16),
        ],
        scratch_shapes=[
            pltpu.VMEM((wide, members * fields), bf16),
            pltpu.VMEM((grid_rows, wide), bf16),
            pltpu.VMEM((fields, grid_rows), bf16),
            pltpu.VMEM((fields, tok_rows), f32),
            pltpu.VMEM((2, fields, REACH), bf16),
            pltpu.VMEM((2, fields, REACH), bf16),
            pltpu.VMEM((2, members, seqs, chunk, fields), bf16),
            pltpu.VMEM((2, members, seqs, chunk, fields), bf16),
            pltpu.VMEM((2, seqs, chunk, fields), bf16),
            pltpu.VMEM((2, seqs, chunk, fields), bf16),
            pltpu.VMEM((2, chunk, fields), bf16),
            pltpu.VMEM((members, chunk, fields), bf16),
            pltpu.VMEM((peers, chunk, fields), bf16),
            pltpu.VMEM(tokens.shape, bf16),
            pltpu.VMEM(tokens.shape, bf16),
            pltpu.VMEM(observed.shape, f32),
            pltpu.VMEM(output_weight.shape, bf16),
            pltpu.VMEM(weight.shape, bf16),
            pltpu.VMEM(tokens.shape, bf16),
            pltpu.VMEM((WINDOW, width), bf16),
            pltpu.VMEM((tok_rows, 3 * width), bf16),
            pltpu.VMEM((WINDOW, 2 * width), bf16),
            pltpu.VMEM((tok_rows, fields), f32),
            pltpu.VMEM((tok_rows + WINDOW, LANES), bf16),
            pltpu.VMEM((2, tok_rows + WINDOW, LANES), bf16),
            dma((2,)),
            dma((2,)),
            dma((3 + weight.shape[1] // COLS,)),
            dma((members,)),
            dma((members,)),
            dma((2, members)),
            dma((2, members)),
            dma((2,)),
            dma((2,)),
            dma((2, members)),
            dma((2, members)),
            dma((2, seqs)),
            dma((2, seqs)),
            dma((members,)),
            dma((members,)),
            dma((peers,)),
            dma((peers,)),
        ],
        compiler_params=pltpu.CompilerParams(
            vmem_limit_bytes=56 << 20, collective_id=0, has_side_effects=True
        ),
    )(decoder, neighbours, area, tokens, weight, observed, output_weight)


def body(tokens, input_weight, output_weight, decoder_weight, neighbours, observed, cell_area):
    own_tokens = tokens[0]
    tok_rows, width = own_tokens.shape
    fields = decoder_weight.shape[1]
    seqs = lax.axis_size("seq")
    members = lax.axis_size("member")
    grid_rows = neighbours.shape[0]
    middle, rows, decoder_sum, joint = layer(
        decoder_weight, neighbours, cell_area[:, None], own_tokens, input_weight, observed,
        output_weight, seqs, members,
    )
    attention_cotangent = lax.dot_general(
        middle, joint, (((1,), (1,)), ((), ())), preferred_element_type=f32
    ).astype(bf16)
    output_gradient = lax.dot_general(
        rows.reshape(width // seqs, fields), decoder_weight, (((1,), (1,)), ((), ())),
        preferred_element_type=f32,
    ) * (1.0 / math.sqrt(members * tok_rows * seqs))
    decoder_gradient = decoder_sum.reshape(width, fields).astype(f32) * (
        1.0 / math.sqrt(members * grid_rows * seqs)
    )
    return (attention_cotangent[None], output_gradient, decoder_gradient)


def solution(mesh):
    in_specs = (
        P(("group", "member"), "seq", None),
        P(),
        P(),
        P(),
        P("seq", None),
        P(("group", "seq"), None),
        P("seq"),
    )
    out_specs = (P(("group", "member"), "seq", None), P(("group", "seq"), None), P("group", None))
    return jax.shard_map(body, mesh=mesh, in_specs=in_specs, out_specs=out_specs, check_vma=False)
```

time: 84 us -> 79.9 us (0.951)
  Pallas kernels: 63.4 us -> 69.8 us
  starting transfers between devices: 6.37 us -> 0 us
  local copies, waits for them, and re-layouts: 5.52 us -> 3.45 us
  waiting for transfers between devices: 1.48 us -> 0 us
  matrix products: 4.97 us -> 3.7 us
  other arithmetic: 0.93 us -> 1.84 us
    pallas_call x4 -> x1, Pallas kernels: 63.4 us -> 69.8 us  [layer(): pl.pallas_call(functools.partial(layer_kernel, seqs, members), in_specs=[...]
    ppermute x2 -> x0, starting transfers between devices: 6.37 us -> none  [the longest x1 5.08 us: from_sides(): lax.ppermute(cells[rows - width:], 'seq', right)]
    dot_general x1 -> x0, matrix products: 2.29 us -> none  [body(): jnp.dot(output_weight, decoder_weight, preferred_element_type=f32)]
    slice x1 -> x0, local copies, waits for them, and re-layouts: 2.28 us -> none  [from_sides(): cells[:width]]
    broadcast_in_dim x1, local copies, waits for them, and re-layouts: 0.22 us -> 1.71 us  [body(): cell_area[:, None]]
    ppermute x2 -> x0, waiting for transfers between devices: 1.48 us -> none  [the longest x1 1.48 us: from_sides(): lax.ppermute(cells[:width], 'seq', left)]
    unnamed x13 -> x5, local copies, waits for them, and re-layouts: 3.02 us -> 1.75 us
    dot_general x1, matrix products: 1.41 us -> 2.43 us  [body(): lax.dot_general(middle, joint, (((1,), (1,)), ((), ())), preferred_elemen...]
  transfers between devices with their start and end apart: 2 -> 0, of which waited for: 1 -> 0; matrix products, arithmetic and copies ran while one was open for 3% -> 0% of each run, Pallas kernels for 8% -> 0%
where the time goes in v3:
time: 79.9 us; the launch traced here: 79.4 us
  Pallas kernels  69.8 us (87%)
  matrix products  3.7 us (5%)
  local copies, waits for them, and re-layouts  3.45 us (4%)
  other arithmetic  1.84 us (2%)
    pallas_call x1, Pallas kernels, layer(): pl.pallas_call(functools.partial(layer_kernel, seqs, members), in_specs=[...  69.8 us
    dot_general x1, matrix products, body(): lax.dot_general(middle, joint, (((1,), (1,)), ((), ())), preferred_elemen...  2.43 us
    mul x1, other arithmetic, body(): decoder_sum.reshape(width, fields).astype(f32)  1.84 us
    unnamed x5, local copies, waits for them, and re-layouts  1.75 us
    broadcast_in_dim x1, local copies, waits for them, and re-layouts, body(): cell_area[:, None]  1.71 us

profile of v3, /device:TPU:0, one launch (start us, length us, event | category | flops | bytes accessed | tf_op | source)
XLA Modules:
  0.0 79.4 jit_solution(8119164873994450076)
XLA Ops:
  0.6 1.7 %copy.11.neighbours = s32[1024,4]{1,0:T(8,128)} copy(s32[1024,4]{0,1:T(4,128)} %param.11) | data formatting | bytes 32768 | tf_op args[4]
  2.4 1.7 %copy.12.area = f32[1024,1]{1,0:T(8,128)} copy(f32[1024,1]{0,1:T(1,128)} %bitcast.13) | data formatting | bytes 8192 | tf_op jit(solution)/shard_map/broadcast_in_dim | solution.py:532
  4.1 69.8 %shard_map.94 = (bf16[512,128]{1,0:T(8,128)(2,1)}, bf16[4,64,128]{2,1,0:T(8,128)(2,1)}, bf16[16,64,128]{2,1,0:T(8,128)(2,1)}, bf16[1024,128]{1,0:T(8,128)(2,1)}) custom-call(bf16[1024,128]{1,0:T(8,128)(2,1)} %decoder.1, s32[1024,4]{1,0:T(8,128)} %copy.11.neighbours, f32[1024,1]{1,0:T(8,128)} %copy.12.area, bf16[512,1024]{1,0:T(8,128)(2,1)} %bitcast.10, ...), custom_call_target="tpu_custom_call" | custom-call | tf_op jit(solution)/shard_map/pallas_call | solution.py:464
  73.9 0.0 copy-start
  73.9 0.0 copy-start.1
  73.9 1.8 %convert_multiply_fusion = f32[16,64,128]{2,1,0:T(8,128)} fusion(bf16[16,64,128]{2,1,0:T(8,128)(2,1)} %get-tuple-element.10), kind=kLoop, calls=%fused_computation.3 | loop fusion | flops 262144 | bytes 786432 | tf_op jit(solution)/shard_map/mul | solution.py:542
  75.7 2.4 %fusion = bf16[1,512,1024]{2,1,0:T(8,128)(2,1)} fusion(bf16[512,128]{1,0:T(8,128)(2,1)} %get-tuple-element.7, bf16[1024,128]{1,0:T(8,128)(2,1)} %get-tuple-element.8), kind=kOutput, calls=%fused_computation.1 | convolution fusion | flops 134742016 | bytes 1441792 | tf_op jit(solution)/shard_map/dot_general | solution.py:535
  78.1 0.0 copy-done
  78.1 0.0 copy-done.1
  78.2 1.3 %convolution_multiply_fusion = f32[256,1024]{1,0:T(8,128)} fusion(bf16[256,128]{1,0:T(8,128)(2,1)S(1)} %bitcast.12, bf16[1024,128]{1,0:T(8,128)(2,1)S(1)} %copy-done), kind=kOutput, calls=%fused_computation.2 | convolution fusion | flops 67371008 | bytes 1376256 | tf_op jit(solution)/shard_map/dot_general | solution.py:538
Async XLA Ops:
  73.9 4.3 %copy-start = (bf16[1024,128]{1,0:T(8,128)(2,1)S(1)}, bf16[1024,128]{1,0:T(8,128)(2,1)}, u32[]{:S(2)}) copy-start(bf16[1024,128]{1,0:T(8,128)(2,1)} %decoder.1) | copy-start | bytes 786436
  73.9 4.3 %copy-start.1 = (bf16[4,64,128]{2,1,0:T(8,128)(2,1)S(1)}, bf16[4,64,128]{2,1,0:T(8,128)(2,1)}, u32[]{:S(2)}) copy-start(bf16[4,64,128]{2,1,0:T(8,128)(2,1)} %get-tuple-element.9) | copy-start | bytes 196612

commit v4 on v3

--- a/solution.py
+++ b/solution.py
@@ -51,72 +51,70 @@
         out[:, at - first : at - first + COLS] = mixed.astype(bf16)
 
 
-def attend(own, side, joint, attended, mapped, keys, values, has_left, has_right):
+def attend(index, own, side, joint, attended, mapped, keys, values, there):
     half = WINDOW // 2
     rows, width = attended.shape
     first = lax.broadcasted_iota(jnp.int32, (1, LANES), 1) < HEAD_DIM
     block = half
     part_rows = block // 2
-    span = block + WINDOW
     part_span = part_rows + WINDOW
     down = lax.broadcasted_iota(jnp.int32, (part_rows, part_rows), 0)
     across = lax.broadcasted_iota(jnp.int32, (part_rows, part_rows), 1)
     late = across >= down
-    exists = (
-        jnp.where(has_left, 1.0, 0.0).astype(f32), 1.0, jnp.where(has_right, 1.0, 0.0).astype(f32)
-    )
+    start = index * block
+    outside = pl.ds(index * half, half)
+    shift = (half, 0)[index]
+    apart = (0, rows)[index]
+    there = jnp.where(there, 1.0, 0.0).astype(f32)
 
     @pl.loop(0, width // LANES)
     def _(j):
         def at(offset):
             return pl.ds(pl.multiple_of(j * LANES + offset, LANES), LANES)
 
-        keys[:half, :] = side[:half, at(0)]
-        keys[half : half + rows, :] = own[:, at(width)]
-        keys[half + rows :, :] = side[half:, at(0)]
+        keys[shift : shift + rows, :] = own[:, at(width)]
+        keys[apart : apart + half, :] = side[outside, at(0)]
         chunks = (
-            (0, side[:half, at(width)]),
-            (half, own[:, at(2 * width)]),
-            (half + rows, side[half:, at(width)]),
-        )
-        for (begin, part), there in zip(chunks, exists):
-            ones = jnp.full(part.shape, there, f32).astype(bf16)
+            (shift, own[:, at(2 * width)], 1.0),
+            (apart, side[outside, at(width)], there),
+        )
+        for begin, part, real in chunks:
+            ones = jnp.full(part.shape, real, f32).astype(bf16)
             values[0, begin : begin + part.shape[0], :] = jnp.where(first, part, ones)
             values[1, begin : begin + part.shape[0], :] = jnp.where(first, ones, part)
-        for start in range(0, rows, block):
-            query = own[start : start + block, at(0)]
-            here = keys[start : start + span, :]
-            sums = []
-            for head in range(2):
-                part = jnp.where(first == (head == 0), query, jnp.zeros_like(query))
-                scores = lax.dot_general(
-                    part, here, (((1,), (1,)), ((), ())), preferred_element_type=f32
+        query = own[start : start + block, at(0)]
+        here = keys[...]
+        sums = []
+        for head in range(2):
+            part = jnp.where(first == (head == 0), query, jnp.zeros_like(query))
+            scores = lax.dot_general(
+                part, here, (((1,), (1,)), ((), ())), preferred_element_type=f32
+            )
+            lines = []
+            for line in range(2):
+                begin = line * part_rows
+                weights = jnp.exp(
+                    scores[begin : begin + part_rows, begin : begin + part_span]
                 )
-                lines = []
-                for line in range(2):
-                    begin = line * part_rows
-                    weights = jnp.exp(
-                        scores[begin : begin + part_rows, begin : begin + part_span]
-                    )
-                    blank = jnp.zeros((part_rows, part_rows), bf16)
-                    pieces = [
-                        jnp.where(late, weights[:, :part_rows], 0.0).astype(bf16),
-                        weights[:, part_rows : part_span - part_rows].astype(bf16),
-                        jnp.where(late, 0.0, weights[:, part_span - part_rows :]).astype(bf16),
-                    ]
-                    pieces = pieces + [blank] if line == 0 else [blank] + pieces
-                    lines.append(jnp.concatenate(pieces, axis=1))
-                total = jnp.dot(
-                    jnp.concatenate(lines, axis=0),
-                    values[head, start : start + span, :],
-                    preferred_element_type=f32,
-                )
-                sums.append(total / pltpu.roll(total, HEAD_DIM, 1))
-            result = jnp.where(first, sums[0], sums[1]).astype(bf16)
-            attended[start : start + block, at(0)] = result
-            mapped[start : start + block, :] += jnp.dot(
-                result, joint[at(0), :], preferred_element_type=f32
+                blank = jnp.zeros((part_rows, part_rows), bf16)
+                pieces = [
+                    jnp.where(late, weights[:, :part_rows], 0.0).astype(bf16),
+                    weights[:, part_rows : part_span - part_rows].astype(bf16),
+                    jnp.where(late, 0.0, weights[:, part_span - part_rows :]).astype(bf16),
+                ]
+                pieces = pieces + [blank] if line == 0 else [blank] + pieces
+                lines.append(jnp.concatenate(pieces, axis=1))
+            total = jnp.dot(
+                jnp.concatenate(lines, axis=0),
+                values[head],
+                preferred_element_type=f32,
             )
+            sums.append(total / pltpu.roll(total, HEAD_DIM, 1))
+        result = jnp.where(first, sums[0], sums[1]).astype(bf16)
+        attended[start : start + block, at(0)] = result
+        mapped[start : start + block, :] += jnp.dot(
+            result, joint[at(0), :], preferred_element_type=f32
+        )
 
 
 def slope(diff):
@@ -139,7 +137,8 @@
     middle_out, rows_out, decoder_out, joint,
     every, counts, turned, middle, edges, edges_in, terms, terms_in, sums, sums_in, mine,
     gathered_rows, gathered, tokens, attended, observed, output_weight,
-    weight, normed, beside, own_parts, side_parts, mapped, keys, values, halo_send, halo_in,
+    weight, normed, beside, own_parts, side_parts, mapped, keys, values, seen,
+    halo_send, halo_in,
     local_sem, field_send, field_in, side_send, side_in, edge_send, edge_in, term_send, term_in,
     sum_send, sum_in, row_send, row_in, all_send, all_in,
 ):
@@ -147,11 +146,10 @@
     peers = seqs * members
     me = s * members + m
     tok_rows, fields = mapped.shape
-    grid_rows, fan = neighbours.shape
+    fan, grid_rows = neighbours.shape
     wide = tok_rows + 2 * REACH
     width = tokens.shape[1]
     chunk = width // peers
-    own = pl.ds(REACH, tok_rows)
 
     def peer(step):
         flat = lax.rem(me + step, peers)
@@ -219,16 +217,18 @@
     mapped[...] = jnp.dot(tokens[...], decoder[...], preferred_element_type=f32)
     base = s * tok_rows - REACH
     block = 128
+    loads[2 + columns].wait()
 
     @pl.loop(0, grid_rows // block)
     def _(i):
-        rows = pl.ds(pl.multiple_of(i * block, block), block)
-        local = neighbours[rows, :] - base
-        place = lax.broadcasted_iota(jnp.int32, (block, wide), 1)
-        total = jnp.zeros((block, wide), f32)
+        cells = pl.ds(pl.multiple_of(i * block, block), block)
+        local = neighbours[:, cells] - base
+        place = lax.broadcasted_iota(jnp.int32, (wide, block), 0)
+        total = jnp.zeros((wide, block), f32)
         for k in range(fan):
-            total += jnp.where(local[:, k : k + 1] == place, 1.0 / fan, 0.0)
-        counts[rows, :] = total.astype(bf16)
+            total += jnp.where(local[k : k + 1, :] == place, 1.0 / fan, 0.0)
+        counts[:, cells] = total.astype(bf16)
+        seen[:, cells] = observed[cells, :].T
 
     @pl.when(has_left)
     def _():
@@ -242,53 +242,51 @@
 
     normed[...] = normalize(beside[...])
     project(normed, weight, side_parts, width, None)
-    attend(
-        own_parts, side_parts, joint, attended, mapped, keys, values, has_left, has_right
-    )
-    every[own, 0:fields] = mapped[...].astype(bf16)
-
-    def field_copy(step):
-        lanes = pl.ds(step * fields, fields)
-        return copy_to(
-            every.at[own, pl.ds(0, fields)], every.at[own, lanes],
-            field_send.at[step], field_in.at[step], s, lax.rem(m + step, members),
+    def field_copy(index, step):
+        cells = pl.ds(REACH + index * half, half)
+        return copy_to(
+            every.at[pl.ds(0, fields), cells], every.at[pl.ds(step * fields, fields), cells],
+            field_send.at[index, step], field_in.at[index, step], s, lax.rem(m + step, members),
         )
 
     def side_copy(side, step):
-        lanes = pl.ds(step * fields, fields)
         start, land, seq = ((tok_rows, 0, s + 1), (REACH, REACH + tok_rows, s - 1))[side]
         return copy_to(
-            every.at[pl.ds(start, REACH), pl.ds(0, fields)],
-            every.at[pl.ds(land, REACH), lanes],
+            every.at[pl.ds(0, fields), pl.ds(start, REACH)],
+            every.at[pl.ds(step * fields, fields), pl.ds(land, REACH)],
             side_send.at[side, step], side_in.at[side, step], seq, lax.rem(m + step, members),
         )
 
-    for step in range(1, members):
-        field_copy(step).start()
-
-    @pl.when(has_right)
-    def _():
-        for step in range(members):
-            side_copy(0, step).start()
-
-    @pl.when(has_left)
-    def _():
-        for step in range(members):
-            side_copy(1, step).start()
+    for index in range(2):
+        attend(
+            index, own_parts, side_parts, joint, attended, mapped, keys, values,
+            (has_left, has_right)[index],
+        )
+        at = index * half
+        every[:fields, REACH + at : REACH + at + half] = (
+            mapped[at : at + half, :].T.astype(bf16)
+        )
+        for step in range(1, members):
+            field_copy(index, step).start()
+
+        @pl.when((has_left, has_right)[index])
+        def _():
+            for step in range(members):
+                side_copy(1 - index, step).start()
 
     @pl.when(jnp.logical_not(has_left))
     def _():
-        every[:REACH, :] = jnp.zeros((REACH, members * fields), bf16)
+        every[:, :REACH] = jnp.zeros((members * fields, REACH), bf16)
         edges_in[0] = jnp.zeros((fields, REACH), bf16)
 
     @pl.when(jnp.logical_not(has_right))
     def _():
-        every[wide - REACH :, :] = jnp.zeros((REACH, members * fields), bf16)
+        every[:, wide - REACH :] = jnp.zeros((members * fields, REACH), bf16)
         edges_in[1] = jnp.zeros((fields, REACH), bf16)
 
-    loads[2 + columns].wait()
-    for step in range(1, members):
-        field_copy(step).wait()
+    for index in range(2):
+        for step in range(1, members):
+            field_copy(index, step).wait()
 
     @pl.when(has_left)
     def _():
@@ -302,23 +300,26 @@
             side_copy(0, step).wait_send()
             side_copy(1, step).wait_recv()
 
+    block = 256
+
     @pl.loop(0, grid_rows // block)
     def _(i):
-        rows = pl.ds(pl.multiple_of(i * block, block), block)
-        found = jnp.dot(counts[rows, :], every[...], preferred_element_type=f32)
-        mean = found[:, :fields]
-        pairs = jnp.zeros((block, fields), f32)
+        cells = pl.ds(pl.multiple_of(i * block, block), block)
+        found = jnp.dot(every[...], counts[:, cells], preferred_element_type=f32)
+        mean = found[:fields, :]
+        pairs = jnp.zeros((fields, block), f32)
         for step in range(members):
-            pairs += slope(mean - found[:, step * fields : (step + 1) * fields])
-        single = slope(mean - observed[rows, :])
-        result = area[rows, :] * (
-            single * (1.0 / members) - pairs * (1.0 / (members * (members - 1)))
-        )
-        turned[:, rows] = result.T.astype(bf16)
+            pairs += slope(mean - found[step * fields : (step + 1) * fields, :])
+        single = slope(mean - seen[:, cells])
+        turned[:, cells] = (
+            area[:, cells]
+            * (single * (1.0 / members) - pairs * (1.0 / (members * (members - 1))))
+        ).astype(bf16)
 
     def spread(start, size):
-        return jnp.dot(
-            turned[...], counts[:, start : start + size], preferred_element_type=f32
+        return lax.dot_general(
+            turned[...], counts[start : start + size, :], (((1,), (1,)), ((), ())),
+            preferred_element_type=f32,
         )
 
     edges[0] = spread(0, REACH).astype(bf16)
@@ -454,7 +455,7 @@
 def layer(decoder, neighbours, area, tokens, weight, observed, output_weight, seqs, members):
     tok_rows, width = tokens.shape
     fields = decoder.shape[1]
-    grid_rows = neighbours.shape[0]
+    grid_rows = neighbours.shape[1]
     wide = tok_rows + 2 * REACH
     peers = seqs * members
     chunk = width // peers
@@ -472,8 +473,8 @@
             jax.ShapeDtypeStruct((width, fields), bf16),
         ],
         scratch_shapes=[
-            pltpu.VMEM((wide, members * fields), bf16),
-            pltpu.VMEM((grid_rows, wide), bf16),
+            pltpu.VMEM((members * fields, wide), bf16),
+            pltpu.VMEM((wide, grid_rows), bf16),
             pltpu.VMEM((fields, grid_rows), bf16),
             pltpu.VMEM((fields, tok_rows), f32),
             pltpu.VMEM((2, fields, REACH), bf16),
@@ -495,13 +496,14 @@
             pltpu.VMEM((tok_rows, 3 * width), bf16),
             pltpu.VMEM((WINDOW, 2 * width), bf16),
             pltpu.VMEM((tok_rows, fields), f32),
-            pltpu.VMEM((tok_rows + WINDOW, LANES), bf16),
-            pltpu.VMEM((2, tok_rows + WINDOW, LANES), bf16),
+            pltpu.VMEM((WINDOW // 2 + WINDOW, LANES), bf16),
+            pltpu.VMEM((2, WINDOW // 2 + WINDOW, LANES), bf16),
+            pltpu.VMEM((fields, grid_rows), f32),
             dma((2,)),
             dma((2,)),
             dma((3 + weight.shape[1] // COLS,)),
-            dma((members,)),
-            dma((members,)),
+            dma((2, members)),
+            dma((2, members)),
             dma((2, members)),
             dma((2, members)),
             dma((2,)),
@@ -529,7 +531,7 @@
     members = lax.axis_size("member")
     grid_rows = neighbours.shape[0]
     middle, rows, decoder_sum, joint = layer(
-        decoder_weight, neighbours, cell_area[:, None], own_tokens, input_weight, observed,
+        decoder_weight, neighbours.T, cell_area[None, :], own_tokens, input_weight, observed,
         output_weight, seqs, members,
     )
     attention_cotangent = lax.dot_general(

time: 79.9 us -> 73.1 us (0.915)
  Pallas kernels: 69.8 us -> 66.2 us
  local copies, waits for them, and re-layouts: 3.45 us -> 0.01 us
    pallas_call x1, Pallas kernels: 69.8 us -> 66.2 us  [layer(): pl.pallas_call(functools.partial(layer_kernel, seqs, members), in_specs=[...]
    unnamed x5 -> x4, local copies, waits for them, and re-layouts: 1.75 us -> 0.01 us
    broadcast_in_dim x1 -> x0, local copies, waits for them, and re-layouts: 1.71 us -> none  [body(): cell_area[:, None]]
where the time goes in v4:
time: 73.1 us; the launch traced here: 72.4 us
  Pallas kernels  66.2 us (91%)
  matrix products  3.7 us (5%)
  other arithmetic  1.84 us (3%)
    pallas_call x1, Pallas kernels, layer(): pl.pallas_call(functools.partial(layer_kernel, seqs, members), in_specs=[...  66.2 us
    dot_general x1, matrix products, body(): lax.dot_general(middle, joint, (((1,), (1,)), ((), ())), preferred_elemen...  2.43 us
    mul x1, other arithmetic, body(): decoder_sum.reshape(width, fields).astype(f32)  1.84 us

profile of v4, /device:TPU:0, one launch (start us, length us, event | category | flops | bytes accessed | tf_op | source)
XLA Modules:
  0.0 72.4 jit_solution(2070586573382175908)
XLA Ops:
  0.6 66.2 %shard_map.94 = (bf16[512,128]{1,0:T(8,128)(2,1)}, bf16[4,64,128]{2,1,0:T(8,128)(2,1)}, bf16[16,64,128]{2,1,0:T(8,128)(2,1)}, bf16[1024,128]{1,0:T(8,128)(2,1)}) custom-call(bf16[1024,128]{1,0:T(8,128)(2,1)} %decoder.1, s32[4,1024]{1,0:T(4,128)} %bitcast.14, f32[1,1024]{1,0:T(1,128)} %bitcast.15, bf16[512,1024]{1,0:T(8,128)(2,1)} %bitcast.11, ...), custom_call_target="tpu_custom_call" | custom-call | tf_op jit(solution)/shard_map/pallas_call | solution.py:465
  66.8 0.0 copy-start
  66.8 0.0 copy-start.1
  66.9 1.8 %convert_multiply_fusion = f32[16,64,128]{2,1,0:T(8,128)} fusion(bf16[16,64,128]{2,1,0:T(8,128)(2,1)} %get-tuple-element.10), kind=kLoop, calls=%fused_computation.3 | loop fusion | flops 262144 | bytes 786432 | tf_op jit(solution)/shard_map/mul | solution.py:544
  68.7 2.4 %fusion = bf16[1,512,1024]{2,1,0:T(8,128)(2,1)} fusion(bf16[512,128]{1,0:T(8,128)(2,1)} %get-tuple-element.7, bf16[1024,128]{1,0:T(8,128)(2,1)} %get-tuple-element.8), kind=kOutput, calls=%fused_computation.1 | convolution fusion | flops 134742016 | bytes 1441792 | tf_op jit(solution)/shard_map/dot_general | solution.py:537
  71.1 0.0 copy-done
  71.1 0.0 copy-done.1
  71.1 1.3 %convolution_multiply_fusion = f32[256,1024]{1,0:T(8,128)} fusion(bf16[256,128]{1,0:T(8,128)(2,1)S(1)} %bitcast.13, bf16[1024,128]{1,0:T(8,128)(2,1)S(1)} %copy-done), kind=kOutput, calls=%fused_computation.2 | convolution fusion | flops 67371008 | bytes 1376256 | tf_op jit(solution)/shard_map/dot_general | solution.py:540
Async XLA Ops:
  66.8 4.3 %copy-start = (bf16[1024,128]{1,0:T(8,128)(2,1)S(1)}, bf16[1024,128]{1,0:T(8,128)(2,1)}, u32[]{:S(2)}) copy-start(bf16[1024,128]{1,0:T(8,128)(2,1)} %decoder.1) | copy-start | bytes 786436
  66.8 4.3 %copy-start.1 = (bf16[4,64,128]{2,1,0:T(8,128)(2,1)S(1)}, bf16[4,64,128]{2,1,0:T(8,128)(2,1)}, u32[]{:S(2)}) copy-start(bf16[4,64,128]{2,1,0:T(8,128)(2,1)} %get-tuple-element.9) | copy-start | bytes 196612

commit v5 on v4

--- a/solution.py
+++ b/solution.py
@@ -109,8 +109,9 @@
                 values[head],
                 preferred_element_type=f32,
             )
-            sums.append(total / pltpu.roll(total, HEAD_DIM, 1))
-        result = jnp.where(first, sums[0], sums[1]).astype(bf16)
+            sums.append(total)
+        shared = pltpu.roll(jnp.where(first, sums[1], sums[0]), HEAD_DIM, 1)
+        result = (jnp.where(first, sums[0], sums[1]) / shared).astype(bf16)
         attended[start : start + block, at(0)] = result
         mapped[start : start + block, :] += jnp.dot(
             result, joint[at(0), :], preferred_element_type=f32
@@ -134,10 +135,10 @@
 
 def layer_kernel(
     seqs, members, decoder, neighbours, area, tokens_far, weight_far, observed_far, output_far,
-    middle_out, rows_out, decoder_out, joint,
+    cotangent_out, rows_out, decoder_out,
     every, counts, turned, middle, edges, edges_in, terms, terms_in, sums, sums_in, mine,
     gathered_rows, gathered, tokens, attended, observed, output_weight,
-    weight, normed, beside, own_parts, side_parts, mapped, keys, values, seen,
+    weight, normed, beside, own_parts, side_parts, mapped, keys, values, seen, joint,
     halo_send, halo_in,
     local_sem, field_send, field_in, side_send, side_in, edge_send, edge_in, term_send, term_in,
     sum_send, sum_in, row_send, row_in, all_send, all_in,
@@ -395,7 +396,10 @@
     put(1, decoder_term)
     for step in range(1, members):
         term_copy(1, step).start()
-    middle_out[...] = middle[...].T.astype(bf16)
+    cotangent_out[...] = lax.dot_general(
+        middle[...].T.astype(bf16), joint[...], (((1,), (1,)), ((), ())),
+        preferred_element_type=f32,
+    ).astype(bf16)
     for part in range(2):
         for step in range(1, members):
             term_copy(part, step).wait()
@@ -465,12 +469,11 @@
     return pl.pallas_call(
         functools.partial(layer_kernel, seqs, members),
         in_specs=[near] * 3 + [far] * 4,
-        out_specs=[near] * 4,
+        out_specs=[near] * 3,
         out_shape=[
-            jax.ShapeDtypeStruct((tok_rows, fields), bf16),
+            jax.ShapeDtypeStruct((tok_rows, width), bf16),
             jax.ShapeDtypeStruct((members, chunk, fields), bf16),
             jax.ShapeDtypeStruct((peers, chunk, fields), bf16),
-            jax.ShapeDtypeStruct((width, fields), bf16),
         ],
         scratch_shapes=[
             pltpu.VMEM((members * fields, wide), bf16),
@@ -499,6 +502,7 @@
             pltpu.VMEM((WINDOW // 2 + WINDOW, LANES), bf16),
             pltpu.VMEM((2, WINDOW // 2 + WINDOW, LANES), bf16),
             pltpu.VMEM((fields, grid_rows), f32),
+            pltpu.VMEM((width, fields), bf16),
             dma((2,)),
             dma((2,)),
             dma((3 + weight.shape[1] // COLS,)),
@@ -530,13 +534,10 @@
     seqs = lax.axis_size("seq")
     members = lax.axis_size("member")
     grid_rows = neighbours.shape[0]
-    middle, rows, decoder_sum, joint = layer(
+    attention_cotangent, rows, decoder_sum = layer(
         decoder_weight, neighbours.T, cell_area[None, :], own_tokens, input_weight, observed,
         output_weight, seqs, members,
     )
-    attention_cotangent = lax.dot_general(
-        middle, joint, (((1,), (1,)), ((), ())), preferred_element_type=f32
-    ).astype(bf16)
     output_gradient = lax.dot_general(
         rows.reshape(width // seqs, fields), decoder_weight, (((1,), (1,)), ((), ())),
         preferred_element_type=f32,

time: 73.1 us -> 74.1 us (1.014)
  local copies, waits for them, and re-layouts: 0.01 us -> 2.27 us
  matrix products: 3.7 us -> 2.11 us
    dot_general x1 -> x0, matrix products: 2.43 us -> none  [body(): lax.dot_general(middle, joint, (((1,), (1,)), ((), ())), preferred_elemen...]
    unnamed x4 -> x3, local copies, waits for them, and re-layouts: 0.01 us -> 2.27 us
    dot_general x1, matrix products: 1.27 us -> 2.11 us  [body(): lax.dot_general(rows.reshape(width // seqs, fields), decoder_weight, (((1...]
where the time goes in v5:
time: 74.1 us; the launch traced here: 73.3 us
  Pallas kernels  66.5 us (90%)
  local copies, waits for them, and re-layouts  2.27 us (3%)
  matrix products  2.11 us (3%)
  other arithmetic  1.8 us (2%)
    pallas_call x1, Pallas kernels, layer(): pl.pallas_call(functools.partial(layer_kernel, seqs, members), in_specs=[...  66.5 us
    unnamed x3, local copies, waits for them, and re-layouts  2.27 us
    dot_general x1, matrix products, body(): lax.dot_general(rows.reshape(width // seqs, fields), decoder_weight, (((1...  2.11 us
    mul x1, other arithmetic, body(): decoder_sum.reshape(width, fields).astype(f32)  1.8 us

profile of v5, /device:TPU:0, one launch (start us, length us, event | category | flops | bytes accessed | tf_op | source)
XLA Modules:
  0.0 73.3 jit_solution(7527920172673923126)
XLA Ops:
  0.6 0.0 copy-start
  0.6 66.5 %shard_map.94 = (bf16[512,1024]{1,0:T(8,128)(2,1)}, bf16[4,64,128]{2,1,0:T(8,128)(2,1)}, bf16[16,64,128]{2,1,0:T(8,128)(2,1)}) custom-call(bf16[1024,128]{1,0:T(8,128)(2,1)} %decoder.1, s32[4,1024]{1,0:T(4,128)} %bitcast.12, f32[1,1024]{1,0:T(1,128)} %bitcast.13, bf16[512,1024]{1,0:T(8,128)(2,1)} %bitcast.8, bf16[1024,3072]{1,0:T(8,128)(2,1)} %weight_far.1, ...), custom_call_target="tpu_custom_call" | custom-call | tf_op jit(solution)/shard_map/pallas_call | solution.py:469
  67.1 1.8 %convert_multiply_fusion = f32[16,64,128]{2,1,0:T(8,128)} fusion(bf16[16,64,128]{2,1,0:T(8,128)(2,1)} %get-tuple-element.8), kind=kLoop, calls=%fused_computation.1 | loop fusion | flops 262144 | bytes 786432 | tf_op jit(solution)/shard_map/mul | solution.py:545
  68.9 0.0 copy-done
  68.9 2.1 %convolution_multiply_fusion = f32[256,1024]{1,0:T(8,128)} fusion(bf16[256,128]{1,0:T(8,128)(2,1)} %bitcast.11, bf16[1024,128]{1,0:T(8,128)(2,1)S(1)} %copy-done), kind=kOutput, calls=%fused_computation | convolution fusion | flops 67371008 | bytes 1376256 | tf_op jit(solution)/shard_map/dot_general | solution.py:541
  71.0 2.3 %copy.11 = bf16[1,512,1024]{2,1,0:T(8,128)(2,1)} copy(bf16[1,512,1024]{2,1,0:T(8,128)(2,1)} %bitcast.9) | data formatting | bytes 2097152
Async XLA Ops:
  0.6 68.3 %copy-start = (bf16[1024,128]{1,0:T(8,128)(2,1)S(1)}, bf16[1024,128]{1,0:T(8,128)(2,1)}, u32[]{:S(2)}) copy-start(bf16[1024,128]{1,0:T(8,128)(2,1)} %decoder.1) | copy-start | bytes 786436
